TPU v7x, 32 devices: a whole 2x2x4 slice. The times are simulated.
32 devices in a mesh: dp: 4 (over y, core), expert: 8 (over z, x).
Axes of the slice: x: 2, y: 2, z: 4, core: 2. Of those that a mesh axis runs over, the one named last changes fastest.
Arguments:
- tokens: bfloat16 [12288, 1024], P(('dp', 'expert')), may hold values from -6 to 6
- cotangent: bfloat16 [12288, 1024], P(('dp', 'expert')), may hold values from -6 to 6
- routes: int32 [12288, 8], P(('dp', 'expert')), may hold values from 0 to 31, all different within a row
- fill_order: int32 [32, 384], P(('dp', 'expert')), may hold values from 0 to 383, each once within a row
- picture_span: int32 [32, 2], P(('dp', 'expert')), may hold values from 0 to 384, as said below
- w_query: bfloat16 [1024, 1024], P('dp'), may hold values from -0.1875 to 0.1875
- w_keyval: bfloat16 [1024, 1024], P('dp'), may hold values from -0.1875 to 0.1875
- w_output: bfloat16 [1024, 1024], P('dp'), may hold values from -1 to 1
- w_router: bfloat16 [1024, 32], P('dp'), may hold values from -0.09375 to 0.09375
- gain_attn: bfloat16 [1024], P('dp'), may hold values from 0.5 to 1.5
- gain_moe: bfloat16 [1024], P('dp'), may hold values from 0.5 to 1.5
- w_gate_up: bfloat16 [32, 1024, 1024], P('expert'), may hold values from -0.1875 to 0.1875
- w_down: bfloat16 [32, 512, 1024], P('expert'), may hold values from -0.75 to 0.75
Outputs:
- output: bfloat16 [12288, 1024], P(('dp', 'expert'))
- grad_tokens: float32 [12288, 1024], P(('dp', 'expert'))
- grad_w_query: float32 [1024, 1024], P('dp')
- grad_w_keyval: float32 [1024, 1024], P('dp')
- grad_w_output: float32 [1024, 1024], P('dp')
- grad_w_router: float32 [1024, 32], P('dp')
- grad_gain_attn: float32 [1024], P('dp')
- grad_gain_moe: float32 [1024], P('dp')
- grad_w_gate_up: float32 [32, 1024, 1024], P('expert')
- grad_w_down: float32 [32, 512, 1024], P('expert')
Inputs may be any that keep to these rules, and one draw needn't show every extreme that they name: `routes`: each row names 8 different experts. `fill_order`: each row holds every position of one sequence once. picture_span[s, 1] = picture_span[s, 0] + 256.
All inputs are finite; a program needn't handle non-finite values.
Results may differ from a plain program's by a relative error of at most 0.02.
Values may be sent and summed in bfloat16 or wider, within the bound.
A program may use at most 256 MiB of HBM per device.

v0:
```python
import math

import jax
import jax.numpy as jnp
from jax import lax
from jax.sharding import PartitionSpec as P

HEADS = 16
KV_HEADS = 8
HEAD_DIM = 64
EXPERTS = 32
EXP_FF = 512
TOP = 8
CAP = 108


norm_eps = 1e-05
rope_theta = 10000.0
excluded = -1e30


def rms_inverse(values):
    return lax.rsqrt(jnp.mean(values * values, axis=-1, keepdims=True) + norm_eps)


def norm_back(grad_act, normed, inverse, gain_vec):
    scaled = grad_act * gain_vec
    gain_grad = jnp.sum(grad_act * normed, axis=0)
    return (
        inverse * (scaled - normed * jnp.mean(scaled * normed, axis=-1, keepdims=True)),
        gain_grad,
    )


def softmax_rows(values):
    row_max = jnp.max(values, axis=-1, keepdims=True)
    powers = jnp.exp(values - row_max)
    return powers / jnp.sum(powers, axis=-1, keepdims=True)


def rope_tables(seq_len, head_size):
    half_size = head_size // 2
    exponent = jnp.arange(half_size, dtype=jnp.float32) * (2.0 / head_size)
    frequency = rope_theta ** (-exponent)
    angles = jnp.arange(seq_len, dtype=jnp.float32)[:, None] * frequency[None, :]
    return (jnp.cos(angles), jnp.sin(angles))


def rotate(values, cosine, sine_table):
    half_size = values.shape[-1] // 2
    front_part = values[..., :half_size]
    back_part = values[..., half_size:]
    cos_b = cosine[:, None, :]
    sin_b = sine_table[:, None, :]
    return jnp.concatenate(
        [front_part * cos_b - back_part * sin_b, back_part * cos_b + front_part * sin_b], axis=-1
    )


def allowed_mask(seq_len, picture):
    position = jnp.arange(seq_len, dtype=jnp.int32)
    causal = position[None, :] <= position[:, None]
    inside = (position >= picture[0]) & (position < picture[1])
    return causal | inside[:, None] & inside[None, :]


def pair_slots(routes_seq, fill_rows):
    ordered = routes_seq[fill_rows].reshape(-1)
    expert_hot = (ordered[:, None] == jnp.arange(EXPERTS, dtype=jnp.int32)[None, :]).astype(
        jnp.int32
    )
    running = jnp.cumsum(expert_hot, axis=0, dtype=jnp.int32) - 1
    ordered_slot = jnp.sum(running * expert_hot, axis=1, dtype=jnp.int32).reshape(
        fill_rows.shape[0], -1
    )
    return jnp.zeros_like(ordered_slot).at[fill_rows].set(ordered_slot)


def attention_scores(queries, key_rows, allowed, scale_factor):
    raw_scores = jnp.einsum("qkgd,skd->kgqs", queries, key_rows, preferred_element_type=jnp.float32)
    return jnp.where(allowed, raw_scores * scale_factor, excluded)


def swiglu(gate_up):
    gate_part = gate_up[..., :EXP_FF]
    up_part = gate_up[..., EXP_FF:]
    return (gate_part * jax.nn.sigmoid(gate_part) * up_part).astype(jnp.bfloat16)


def shards(
    tokens,
    cotangent,
    routes,
    fill_order,
    picture_span,
    w_query,
    w_keyval,
    w_output,
    w_router,
    gain_attn,
    gain_moe,
    w_gate_up,
    w_down,
):
    query_all, keyval_all, output_all, router_all, gain_one, gain_two = (
        lax.all_gather(w_query, "dp", axis=0, tiled=True),
        lax.all_gather(w_keyval, "dp", axis=0, tiled=True),
        lax.all_gather(w_output, "dp", axis=0, tiled=True),
        lax.all_gather(w_router, "dp", axis=0, tiled=True),
        lax.all_gather(gain_attn, "dp", axis=0, tiled=True),
        lax.all_gather(gain_moe, "dp", axis=0, tiled=True),
    )
    seq_len, width_model = tokens.shape
    group_size = HEADS // KV_HEADS
    kv_cols = KV_HEADS * HEAD_DIM
    scale_factor = 1.0 / math.sqrt(HEAD_DIM)
    inputs = tokens.astype(jnp.float32)
    inverse_one = rms_inverse(inputs)
    normed_one = inputs * inverse_one
    gain_one_f = gain_one.astype(jnp.float32)
    act_one = (normed_one * gain_one_f).astype(jnp.bfloat16)
    query_lin = jnp.dot(act_one, query_all, preferred_element_type=jnp.float32)
    keyval_lin = jnp.dot(act_one, keyval_all, preferred_element_type=jnp.float32)
    cosine, sine_table = rope_tables(seq_len, HEAD_DIM)
    queries = rotate(query_lin.reshape(seq_len, HEADS, HEAD_DIM), cosine, sine_table).astype(
        jnp.bfloat16
    )
    queries = queries.reshape(seq_len, KV_HEADS, group_size, HEAD_DIM)
    key_rows = rotate(
        keyval_lin[:, :kv_cols].reshape(seq_len, KV_HEADS, HEAD_DIM), cosine, sine_table
    ).astype(jnp.bfloat16)
    values = keyval_lin[:, kv_cols:].reshape(seq_len, KV_HEADS, HEAD_DIM).astype(jnp.bfloat16)
    allowed = allowed_mask(seq_len, picture_span[0])
    scores = attention_scores(queries, key_rows, allowed, scale_factor)
    row_max = jnp.max(scores, axis=-1, keepdims=True)
    powers = jnp.exp(scores - row_max)
    row_total = jnp.sum(powers, axis=-1, keepdims=True)
    attention = powers / row_total
    log_total = row_max + jnp.log(row_total)
    attended = jnp.einsum(
        "kgqs,skd->qkgd", attention.astype(jnp.bfloat16), values, preferred_element_type=jnp.float32
    )
    attended = attended.reshape(seq_len, HEADS * HEAD_DIM).astype(jnp.bfloat16)
    hidden = inputs + jnp.dot(attended, output_all, preferred_element_type=jnp.float32)
    inverse_two = rms_inverse(hidden)
    normed_two = hidden * inverse_two
    gain_two_f = gain_two.astype(jnp.float32)
    act_two = (normed_two * gain_two_f).astype(jnp.bfloat16)
    logits = jnp.dot(act_two, router_all, preferred_element_type=jnp.float32)
    route_hot = (routes[:, :, None] == jnp.arange(EXPERTS, dtype=jnp.int32)[None, None, :]).astype(
        jnp.float32
    )
    chosen = jnp.sum(route_hot * logits[:, None, :], axis=-1)
    gate_probs = softmax_rows(chosen)
    pair_slot = pair_slots(routes, fill_order[0])
    kept_pair = (pair_slot < CAP).astype(jnp.float32)
    pair_weight = gate_probs * kept_pair
    flat_expert = routes.reshape(-1)
    flat_slot = pair_slot.reshape(-1)
    clipped = jnp.minimum(flat_slot, CAP - 1)
    dispatch = jnp.zeros((EXPERTS, CAP, width_model), jnp.bfloat16)
    dispatch = dispatch.at[flat_expert, flat_slot].set(
        jnp.repeat(act_two, TOP, axis=0), mode="drop"
    )
    received = lax.all_to_all(dispatch, "expert", split_axis=0, concat_axis=1, tiled=True)
    gate_up = jnp.einsum("erd,edf->erf", received, w_gate_up, preferred_element_type=jnp.float32)
    inner_act = swiglu(gate_up)
    expert_out = jnp.einsum(
        "erf,efd->erd", inner_act, w_down, preferred_element_type=jnp.float32
    ).astype(jnp.bfloat16)
    returned = lax.all_to_all(expert_out, "expert", split_axis=1, concat_axis=0, tiled=True)
    pair_out = returned[flat_expert, clipped].reshape(seq_len, TOP, width_model)
    mixture = jnp.einsum("tk,tkd->td", pair_weight, pair_out, preferred_element_type=jnp.float32)
    output = (hidden + mixture).astype(jnp.bfloat16)
    grad_out = cotangent.astype(jnp.float32)
    pair_grad = (
        jnp.einsum("td,tkd->tk", grad_out, pair_out, preferred_element_type=jnp.float32) * kept_pair
    )
    chosen_grad = gate_probs * (pair_grad - jnp.sum(gate_probs * pair_grad, axis=1, keepdims=True))
    logit_grad = jnp.sum(route_hot * chosen_grad[:, :, None], axis=1).astype(jnp.bfloat16)
    grad_rows = (
        (pair_weight[:, :, None] * grad_out[:, None, :])
        .astype(jnp.bfloat16)
        .reshape(seq_len * TOP, width_model)
    )
    grad_buffer = jnp.zeros_like(dispatch).at[flat_expert, flat_slot].set(grad_rows, mode="drop")
    grad_expert = lax.all_to_all(grad_buffer, "expert", split_axis=0, concat_axis=1, tiled=True)
    inner_grad = jnp.einsum("erd,efd->erf", grad_expert, w_down, preferred_element_type=jnp.float32)
    grad_down = jnp.einsum(
        "erf,erd->efd", inner_act, grad_expert, preferred_element_type=jnp.float32
    )
    gate_part = gate_up[..., :EXP_FF]
    up_part = gate_up[..., EXP_FF:]
    sigmoid_gate = jax.nn.sigmoid(gate_part)
    gate_grad = inner_grad * up_part * sigmoid_gate * (1.0 + gate_part * (1.0 - sigmoid_gate))
    up_grad = inner_grad * gate_part * sigmoid_gate
    gate_up_grad = jnp.concatenate([gate_grad, up_grad], axis=-1).astype(jnp.bfloat16)
    grad_gate_up = jnp.einsum(
        "erd,erf->edf", received, gate_up_grad, preferred_element_type=jnp.float32
    )
    input_grad = jnp.einsum(
        "erf,edf->erd", gate_up_grad, w_gate_up, preferred_element_type=jnp.float32
    ).astype(jnp.bfloat16)
    grad_back = lax.all_to_all(input_grad, "expert", split_axis=1, concat_axis=0, tiled=True)
    pair_input_grad = grad_back[flat_expert, clipped].reshape(seq_len, TOP, width_model)
    act_two_grad = jnp.einsum(
        "tk,tkd->td", kept_pair, pair_input_grad, preferred_element_type=jnp.float32
    )
    act_two_grad = act_two_grad + jnp.dot(
        logit_grad, router_all.T, preferred_element_type=jnp.float32
    )
    grad_router = jnp.dot(act_two.T, logit_grad, preferred_element_type=jnp.float32)
    norm_grad_two, grad_gain_two = norm_back(act_two_grad, normed_two, inverse_two, gain_two_f)
    hidden_grad = grad_out + norm_grad_two
    attn_grad = hidden_grad.astype(jnp.bfloat16)
    grad_output_w = jnp.dot(attended.T, attn_grad, preferred_element_type=jnp.float32)
    attended_grad = jnp.dot(attn_grad, output_all.T, preferred_element_type=jnp.float32).astype(
        jnp.bfloat16
    )
    attended_grad = attended_grad.reshape(seq_len, KV_HEADS, group_size, HEAD_DIM)
    scores_again = attention_scores(queries, key_rows, allowed, scale_factor)
    attention_again = jnp.exp(scores_again - log_total)
    prob_grad = jnp.einsum(
        "qkgd,skd->kgqs", attended_grad, values, preferred_element_type=jnp.float32
    )
    row_dot = jnp.sum(attention_again * prob_grad, axis=-1, keepdims=True)
    score_grad = (attention_again * (prob_grad - row_dot) * scale_factor).astype(jnp.bfloat16)
    query_grad = jnp.einsum(
        "kgqs,skd->qkgd", score_grad, key_rows, preferred_element_type=jnp.float32
    )
    key_grad = jnp.einsum("kgqs,qkgd->skd", score_grad, queries, preferred_element_type=jnp.float32)
    value_grad = jnp.einsum(
        "kgqs,qkgd->skd",
        attention_again.astype(jnp.bfloat16),
        attended_grad,
        preferred_element_type=jnp.float32,
    )
    query_lin_grad = rotate(query_grad.reshape(seq_len, HEADS, HEAD_DIM), cosine, -sine_table)
    query_lin_grad = query_lin_grad.reshape(seq_len, HEADS * HEAD_DIM).astype(jnp.bfloat16)
    key_lin_grad = rotate(key_grad, cosine, -sine_table).reshape(seq_len, kv_cols)
    keyval_lin_grad = jnp.concatenate(
        [key_lin_grad, value_grad.reshape(seq_len, kv_cols)], axis=1
    ).astype(jnp.bfloat16)
    grad_query = jnp.dot(act_one.T, query_lin_grad, preferred_element_type=jnp.float32)
    grad_keyval = jnp.dot(act_one.T, keyval_lin_grad, preferred_element_type=jnp.float32)
    act_one_grad = jnp.dot(query_lin_grad, query_all.T, preferred_element_type=jnp.float32)
    act_one_grad = act_one_grad + jnp.dot(
        keyval_lin_grad, keyval_all.T, preferred_element_type=jnp.float32
    )
    norm_grad_one, grad_gain_one = norm_back(act_one_grad, normed_one, inverse_one, gain_one_f)
    grad_tokens = hidden_grad + norm_grad_one
    local_grads = (
        grad_query,
        grad_keyval,
        grad_output_w,
        grad_router,
        grad_gain_one,
        grad_gain_two,
    )
    shares = (
        lax.psum_scatter(
            local_grads[0].astype(jnp.bfloat16), "dp", scatter_dimension=0, tiled=True
        ).astype(jnp.float32),
        lax.psum_scatter(
            local_grads[1].astype(jnp.bfloat16), "dp", scatter_dimension=0, tiled=True
        ).astype(jnp.float32),
        lax.psum_scatter(
            local_grads[2].astype(jnp.bfloat16), "dp", scatter_dimension=0, tiled=True
        ).astype(jnp.float32),
        lax.psum_scatter(
            local_grads[3].astype(jnp.bfloat16), "dp", scatter_dimension=0, tiled=True
        ).astype(jnp.float32),
        lax.psum_scatter(
            local_grads[4].astype(jnp.bfloat16), "dp", scatter_dimension=0, tiled=True
        ).astype(jnp.float32),
        lax.psum_scatter(
            local_grads[5].astype(jnp.bfloat16), "dp", scatter_dimension=0, tiled=True
        ).astype(jnp.float32),
    )
    summed = (
        lax.psum(shares[0].astype(jnp.bfloat16), "expert").astype(jnp.float32),
        lax.psum(shares[1].astype(jnp.bfloat16), "expert").astype(jnp.float32),
        lax.psum(shares[2].astype(jnp.bfloat16), "expert").astype(jnp.float32),
        lax.psum(shares[3].astype(jnp.bfloat16), "expert").astype(jnp.float32),
        lax.psum(shares[4].astype(jnp.bfloat16), "expert").astype(jnp.float32),
        lax.psum(shares[5].astype(jnp.bfloat16), "expert").astype(jnp.float32),
    )
    expert_summed = (
        lax.psum(grad_gate_up.astype(jnp.bfloat16), "dp").astype(jnp.float32),
        lax.psum(grad_down.astype(jnp.bfloat16), "dp").astype(jnp.float32),
    )
    return (
        output,
        grad_tokens,
        summed[0],
        summed[1],
        summed[2],
        summed[3],
        summed[4],
        summed[5],
        expert_summed[0],
        expert_summed[1],
    )


def solution(mesh):
    return jax.shard_map(
        shards,
        mesh=mesh,
        in_specs=(
            P(("dp", "expert"), None),
            P(("dp", "expert"), None),
            P(("dp", "expert"), None),
            P(("dp", "expert"), None),
            P(("dp", "expert"), None),
            P("dp", None),
            P("dp", None),
            P("dp", None),
            P("dp", None),
            P("dp"),
            P("dp"),
            P("expert", None, None),
            P("expert", None, None),
        ),
        out_specs=(
            P(("dp", "expert"), None),
            P(("dp", "expert"), None),
            P("dp", None),
            P("dp", None),
            P("dp", None),
            P("dp", None),
            P("dp"),
            P("dp"),
            P("expert", None, None),
            P("expert", None, None),
        ),
        check_vma=False,
    )
```

profile of v0, /device:TPU:0, one launch (start us, length us, event | category | flops | bytes accessed | tf_op | source)
XLA Modules:
  0.0 1560.6 jit_solution(5390979081941771722)
XLA Ops:
  30.5 9.2 reduce-window.6
  46.1 13.0 all-gather.8.cloned.1.call-done
  71.0 12.3 all-gather.10.cloned.1.call-done
  87.3 18.9 %scatter_custom_fusion.1 = bf16[3456,1024]{1,0:T(8,128)(2,1)} fusion(s32[3072]{0:T(1024)S(1)} %broadcast_select_fusion, bf16[]{:T(256)} %constant.45.clone.1, bf16[384,1024]{1,0:T(8,128)(2,1)S(1)} %multiply_convert_fusion.3), kind=kCustom, calls=%fused_computation.35 | custom fusion | bytes 7864322
  113.2 166.4 %all_to_all.72 = bf16[32,108,1024]{2,1,0:T(8,128)(2,1)} all-to-all(bf16[32,108,1024]{2,1,0:T(8,128)(2,1)S(1)} %copy.167), channel_id=1, replica_groups=mesh['dp'=4,'expert'=8] {'expert'}, dimensions={0} | all-to-all | bytes 14155776 | tf_op jit(solution)/shard_map/all_to_all | solution.py:165
  287.1 8.7 all_to_all.55
  295.7 10.9 fusion.101
  324.5 11.4 copy.169
  347.1 148.0 %all-to-all-done.1 = bf16[4,864,1024]{2,0,1:T(4,128)(2,1)} async-done(((bf16[4,864,1024]{2,0,1:T(4,128)(2,1)}), bf16[4,864,1024]{2,0,1:T(4,128)(2,1)}, u32[]{:S(2)}, u32[]{:S(2)}) %all-to-all-start.1) | async-done | bytes 7077920 | tf_op jit(solution)/shard_map/all_to_all | solution.py:171
  495.1 8.5 copy.209
  503.6 11.4 copy.171
  514.9 12.4 all_to_all.59
  527.3 62.6 %gather_fusion.1 = bf16[3072,1024]{1,0:T(8,128)(2,1)} fusion(bf16[32,108,1024]{2,0,1:T(8,128)(2,1)} %all_to_all.59, s32[3072]{0:T(1024)S(1)} %bitcast.217), kind=kCustom, calls=%fused_computation.1 | custom fusion | bytes 12607488 | tf_op jit(solution)/shard_map/gather | solution.py:172
  596.7 19.8 %scatter_custom_fusion.2 = bf16[3456,1024]{1,0:T(8,128)(2,1)} fusion(s32[3072]{0:T(1024)S(1)} %broadcast_select_fusion, f32[384,1024]{1,0:T(8,128)S(1)} %convert_element_type.155, f32[3072]{0:T(1024)S(1)} %mul.495, bf16[]{:T(256)} %constant.45.clone.1), kind=kCustom, calls=%fused_computation.28 | custom fusion | flops 6291456 | bytes 8663042
  623.6 164.2 %all_to_all.73 = bf16[32,108,1024]{2,1,0:T(8,128)(2,1)} all-to-all(bf16[32,108,1024]{2,1,0:T(8,128)(2,1)S(1)} %copy.173), channel_id=1, replica_groups=mesh['dp'=4,'expert'=8] {'expert'}, dimensions={0} | all-to-all | bytes 14155776 | tf_op jit(solution)/shard_map/all_to_all | solution.py:187
  795.3 8.7 all_to_all.63
  804.0 13.2 multiply_convert_fusion.1
  817.2 14.4 convolution_convert_fusion.1
  831.6 11.4 copy.175
  853.1 148.8 %all-to-all-done.3 = bf16[4,864,1024]{2,0,1:T(4,128)(2,1)} async-done(((bf16[4,864,1024]{2,0,1:T(4,128)(2,1)}), bf16[4,864,1024]{2,0,1:T(4,128)(2,1)}, u32[]{:S(2)}, u32[]{:S(2)}) %all-to-all-start.3) | async-done | bytes 7077920 | tf_op jit(solution)/shard_map/all_to_all | solution.py:204
  1010.3 11.5 copy.177
  1021.8 12.1 all_to_all.67
  1034.0 62.5 %gather_fusion.2 = bf16[3072,1024]{1,0:T(8,128)(2,1)} fusion(bf16[32,108,1024]{2,0,1:T(8,128)(2,1)} %all_to_all.67, s32[3072]{0:T(1024)S(1)} %bitcast.218), kind=kCustom, calls=%fused_computation.2 | custom fusion | bytes 12607488 | tf_op jit(solution)/shard_map/gather | solution.py:205
  1115.2 18.2 %fusion.44 = f32[384,8,64]{0,2,1:T(8,128)S(1)} fusion(f32[8,384,384,2]{2,1,3,0:T(8,128)} %fusion.102, f32[8,2,384]{2,1,0:T(2,128)S(1)} %bitcast.253, f32[8,384,384,2]{2,1,3,0:T(8,128)} %copy-done.5, pred[384,384]{0,1:T(8,128)(4,1)S(1)} %copy-done.20, bf16[384,8,2,32]{0,3,2,1:T(8,128)(2,1)} %bitcast.241, bf16[384,8,2,32]{0,3,2,1:T(8,128)(2,1)} %bitcast.239), kind=kOutput, calls=%fused_computation.81 | convolution fusion | flops 329521536 | bytes 20619264 | tf_op jit(solution)/shard_map/kgqs,qkgd->skd/dot_general | solution.py:231
  1143.4 18.7 %fusion.33 = f32[8,64,2,384]{3,1,2,0:T(8,128)} fusion(f32[8,384,384,2]{2,1,3,0:T(8,128)} %fusion.102, f32[8,2,384]{2,1,0:T(2,128)S(1)} %bitcast.255, f32[8,384,384,2]{2,1,3,0:T(8,128)} %copy-done.5, pred[384,384]{0,1:T(8,128)(4,1)S(1)} %copy-done.20, bf16[384,8,32]{0,2,1:T(8,128)(2,1)S(1)} %copy-done.31, bf16[384,8,32]{0,2,1:T(8,128)(2,1)S(1)} %copy-done.29), kind=kOutput, calls=%fused_computation.61 | convolution fusion | flops 328735104 | bytes 21012480 | tf_op jit(solution)/shard_map/kgqs,skd->qkgd/dot_general | solution.py:228
  1167.9 10.8 convolution_convert_fusion.3
  1178.7 14.5 convolution_convert_fusion
  1195.6 11.0 reduce-scatter.5.cloned.1.call-done
  1207.9 222.7 %all-reduce.11.cloned.1.call-done = (bf16[4,1024,1024]{2,1,0:T(8,128)(2,1)}, bf16[4,512,1024]{2,1,0:T(8,128)(2,1)}) async-done(((bf16[4,1024,1024]{2,1,0:T(8,128)(2,1)}, bf16[4,512,1024]{2,1,0:T(8,128)(2,1)}), (bf16[4,1024,1024]{2,1,0:T(8,128)(2,1)}, bf16[4,512,1024]{2,1,0:T(8,128)(2,1)})) %all-reduce.11.cloned.1.call-update) | async-done | bytes 12582928 | tf_op jit(solution)/shard_map/psum | solution.py:289
  1430.6 11.7 convert_element_type.177
  1459.4 38.3 %all-reduce.2 = (bf16[256,32]{0,1:T(8,128)(2,1)S(1)}, bf16[256]{0:T(256)(128)(2,1)S(1)}, bf16[256]{0:T(256)(128)(2,1)S(1)}) all-reduce(bf16[256,32]{0,1:T(8,128)(2,1)} %reduce-scatter.11.cloned.1.call-done, bf16[256]{0:T(256)(128)(2,1)S(1)} %dynamic-slice.1, ...), channel_id=1, replica_groups=mesh['dp'=4,'expert'=8] {'expert'}, use_global_device_ids=true, to_apply=%region_25.26 | all-reduce | flops 8704 | bytes 34816 | tf_op jit(solution)/shard_map/psum | solution.py:284
  1502.5 44.8 %all-reduce.9.cloned.1.call-done = (bf16[256,1024]{1,0:T(8,128)(2,1)}, bf16[256,1024]{1,0:T(8,128)(2,1)}, bf16[256,1024]{1,0:T(8,128)(2,1)}) async-done(((bf16[256,1024]{1,0:T(8,128)(2,1)}, bf16[256,1024]{1,0:T(8,128)(2,1)}, bf16[256,1024]{1,0:T(8,128)(2,1)}), (bf16[256,1024]{1,0:T(8,128)(2,1)}, bf16[256,1024]{1,0:T(8,128)(2,1)}, bf16[256,1024]{1,0:T(8,128)(2,1)})) %all-reduce.9.cloned.1.call-update) | async-done | bytes 1572880 | tf_op jit(solution)/shard_map/psum | solution.py:281
  (237 shorter events, 193.8 us)
Async XLA Ops:
  7.2 35.3 %copy-start.48 = (s32[2]{0:T(128)S(1)}, s32[2]{0:T(128)}, u32[]{:S(2)}) copy-start(s32[2]{0:T(128)} %constant.56) | copy-start | bytes 28
  7.2 35.4 %copy-start.47 = (s32[2]{0:T(128)S(1)}, s32[2]{0:T(128)}, u32[]{:S(2)}) copy-start(s32[2]{0:T(128)} %constant.53) | copy-start | bytes 28
  7.2 35.5 %copy-start.6 = (bf16[384,1024]{1,0:T(8,128)(2,1)S(1)}, bf16[384,1024]{1,0:T(8,128)(2,1)}, u32[]{:S(2)}) copy-start(bf16[384,1024]{1,0:T(8,128)(2,1)} %param.13) | copy-start | bytes 2359300
  7.2 35.5 %all-gather.6.cloned.1.call-start = ((), (), s32[]{:S(2)}) async-start(), calls=%async_computation.8 | async-start | bytes 2621440 | tf_op jit(solution)/shard_map/all_gather | solution.py:107
  7.9 51.2 %all-gather.8.cloned.1.call-start = ((), (), s32[]{:S(2)}) async-start(), calls=%async_computation.9 | async-start | bytes 2621440 | tf_op jit(solution)/shard_map/all_gather | solution.py:106
  8.7 74.6 %all-gather.10.cloned.1.call-start = ((), (), s32[]{:S(2)}) async-start(), calls=%async_computation.10 | async-start | bytes 2621440 | tf_op jit(solution)/shard_map/all_gather | solution.py:108
  16.5 42.6 %copy-start.45 = (f32[384]{0:T(512)}, f32[384]{0:T(512)S(1)}, u32[]{:S(2)}) copy-start(f32[384]{0:T(512)S(1)} %add_rsqrt_fusion.1) | copy-start | bytes 4612
  22.6 63.4 %copy-start.37 = (f32[4,1,256]{2,1,0:T(1,128)}, f32[4,1,256]{2,1,0:T(1,128)S(1)}, u32[]{:S(2)}) copy-start(f32[4,1,256]{2,1,0:T(1,128)S(1)} %convert_element_type.181) | copy-start | bytes 12292
  28.1 31.0 %copy-start.43 = (f32[4,1,256]{2,1,0:T(1,128)}, f32[4,1,256]{2,1,0:T(1,128)S(1)}, u32[]{:S(2)}) copy-start(f32[4,1,256]{2,1,0:T(1,128)S(1)} %convert_element_type.180) | copy-start | bytes 12292
  29.6 36.5 %copy-start.19 = (pred[384,384]{0,1:T(8,128)(4,1)}, pred[384,384]{0,1:T(8,128)(4,1)S(1)}, u32[]{:S(2)}) copy-start(pred[384,384]{0,1:T(8,128)(4,1)S(1)} %fusion.51) | copy-start | bytes 442372
  30.5 31.8 %copy-start.15 = (f32[384,32]{0,1:T(8,128)}, f32[384,32]{0,1:T(8,128)S(1)}, u32[]{:S(2)}) copy-start(f32[384,32]{0,1:T(8,128)S(1)} %get-tuple-element.45) | copy-start | bytes 147460
  46.1 20.0 %copy-start.13 = (bf16[384,512]{0,1:T(8,128)(2,1)}, bf16[384,512]{0,1:T(8,128)(2,1)S(1)}, u32[]{:S(2)}) copy-start(bf16[384,512]{0,1:T(8,128)(2,1)S(1)} %copy.158) | copy-start | bytes 1179652
  71.0 35.2 %copy-start.11 = (bf16[8,64,2,384]{3,1,2,0:T(8,128)(2,1)}, bf16[8,64,2,384]{3,1,2,0:T(8,128)(2,1)S(1)}, u32[]{:S(2)}) copy-start(bf16[8,64,2,384]{3,1,2,0:T(8,128)(2,1)S(1)} %fusion.43) | copy-start | bytes 2359300
  86.0 27.2 %copy-start.39 = (f32[384]{0:T(512)}, f32[384]{0:T(512)S(1)}, u32[]{:S(2)}) copy-start(f32[384]{0:T(512)S(1)} %add_rsqrt_fusion) | copy-start | bytes 4612
  87.3 259.3 %copy-start.3 = (bf16[384,1024]{1,0:T(8,128)(2,1)}, bf16[384,1024]{1,0:T(8,128)(2,1)S(1)}, u32[]{:S(2)}) copy-start(bf16[384,1024]{1,0:T(8,128)(2,1)S(1)} %multiply_convert_fusion.3) | copy-start | bytes 2359300
  335.9 11.0 copy-start.32
  335.9 159.2 %all-to-all-start.1 = ((bf16[4,864,1024]{2,0,1:T(4,128)(2,1)}), bf16[4,864,1024]{2,0,1:T(4,128)(2,1)}, u32[]{:S(2)}, u32[]{:S(2)}) async-start(bf16[4,864,1024]{2,0,1:T(4,128)(2,1)} %copy.169), calls=%async_computation.1 | async-start | bytes 14155776 | tf_op jit(solution)/shard_map/all_to_all | solution.py:171
  843.0 158.8 %all-to-all-start.3 = ((bf16[4,864,1024]{2,0,1:T(4,128)(2,1)}), bf16[4,864,1024]{2,0,1:T(4,128)(2,1)}, u32[]{:S(2)}, u32[]{:S(2)}) async-start(bf16[4,864,1024]{2,0,1:T(4,128)(2,1)} %copy.175), calls=%async_computation.3 | async-start | bytes 14155776 | tf_op jit(solution)/shard_map/all_to_all | solution.py:204
  847.8 347.8 %reduce-scatter.9.cloned.1.call-start = ((), (), s32[]{:S(2)}) async-start(), calls=%async_computation.13 | async-start | bytes 2621440 | tf_op jit(solution)/shard_map/reduce_scatter | solution.py:267
  848.5 252.7 %copy-start.26 = (bf16[384,32]{0,1:T(8,128)(2,1)}, bf16[384,32]{0,1:T(8,128)(2,1)S(1)}, u32[]{:S(2)}) copy-start(bf16[384,32]{0,1:T(8,128)(2,1)S(1)} %select_reduce_fusion) | copy-start | bytes 73732
  1106.3 89.3 %reduce-scatter.7.cloned.1.call-start = ((), (), s32[]{:S(2)}) async-start(), calls=%async_computation.12 | async-start | bytes 2621440 | tf_op jit(solution)/shard_map/reduce_scatter | solution.py:264
  1115.2 18.2 %copy-start.16 = (f32[384,32]{0,1:T(8,128)S(1)}, f32[384,32]{0,1:T(8,128)}, u32[]{:S(2)}) copy-start(f32[384,32]{0,1:T(8,128)} %copy-done.15) | copy-start | bytes 147460
  1115.2 18.2 %copy-start.21 = (f32[384,32]{0,1:T(8,128)S(1)}, f32[384,32]{0,1:T(8,128)}, u32[]{:S(2)}) copy-start(f32[384,32]{0,1:T(8,128)} %get-tuple-element.43) | copy-start | bytes 147460
  1133.5 7.0 copy-start.7
  1133.6 7.0 copy-start.44
  1133.6 6.9 copy-start.46
  1143.3 63.3 %reduce-scatter.5.cloned.1.call-start = ((), (), s32[]{:S(2)}) async-start(), calls=%async_computation.11 | async-start | bytes 2621440 | tf_op jit(solution)/shard_map/reduce_scatter | solution.py:261
  1167.6 263.0 %all-reduce.11.cloned.1.call-start = ((), (), s32[]{:S(2)}) async-start(), calls=%async_computation.16 | async-start | bytes 25165824 | tf_op jit(solution)/shard_map/psum | solution.py:289
  1167.9 10.8 copy-start.54
  1193.2 13.4 copy-start.53
  1193.2 266.1 %reduce-scatter.11.cloned.1.call-start = ((), (), s32[]{:S(2)}) async-start(), calls=%async_computation.14 | async-start | bytes 81920 | tf_op jit(solution)/shard_map/reduce_scatter | solution.py:270
  1195.3 352.0 %all-reduce.9.cloned.1.call-start = ((), (), s32[]{:S(2)}) async-start(), calls=%async_computation.15 | async-start | bytes 3145728 | tf_op jit(solution)/shard_map/psum | solution.py:281
  (34 other events, 127.7 us)
Sparse Core Ops, SparseCore 0:
  9.6 25.3 all-gather.5
  36.5 22.6 all-gather.7
  60.7 22.5 all-gather.9
  1106.4 29.2 reduce-scatter.8
  1143.4 29.5 reduce-scatter.6
  1175.4 31.1 reduce-scatter.4
  1209.8 220.7 all-reduce.10
  1433.6 19.7 reduce-scatter.10
  1457.2 89.9 all-reduce.8
where the time goes:
time: 1570 us; the launch traced here: 1560 us
  waiting for transfers between devices  603 us (38%)
  blocking collectives  392 us (25%)
  local copies, waits for them, and re-layouts  300 us (19%)
  matrix products  166 us (11%)
  other arithmetic  73.2 us (5%)
  between operations  16 us (1%)
    psum x1, waiting for transfers between devices, shards(): lax.psum(grad_gate_up.astype(jnp.bfloat16), 'dp').astype(jnp.float32)  223 us
    all_to_all x1, blocking collectives, shards(): lax.all_to_all(dispatch, 'expert', split_axis=0, concat_axis=1, tiled=True)  166 us
    all_to_all x1, blocking collectives, shards(): lax.all_to_all(grad_buffer, 'expert', split_axis=0, concat_axis=1, tiled=...  164 us
    all_to_all x1, waiting for transfers between devices, shards(): lax.all_to_all(input_grad, 'expert', split_axis=1, concat_axis=0, tiled=T...  149 us
    all_to_all x1, waiting for transfers between devices, shards(): lax.all_to_all(expert_out, 'expert', split_axis=1, concat_axis=0, tiled=T...  148 us
    gather x1, local copies, waits for them, and re-layouts, shards(): pair_out = returned[flat_expert, clipped].reshape(seq_len, TOP, width_model)  62.6 us
    gather x1, local copies, waits for them, and re-layouts, shards(): grad_back[flat_expert, clipped].reshape(seq_len, TOP, width_model)  62.5 us
    psum x1, waiting for transfers between devices, shards(): lax.psum(shares[0].astype(jnp.bfloat16), 'expert').astype(jnp.float32)  44.8 us
  transfers between devices with their start and end apart: 11, of which 7 were waited for; matrix products, arithmetic and copies ran while one was open for 10% of the time, Pallas kernels for 0%

commit v1 on v0

v1 whole, which is shorter than its diff:
```python
import functools
import math

import jax
import jax.numpy as jnp
from jax import lax
from jax.experimental import pallas as pl
from jax.experimental.pallas import tpu as pltpu
from jax.sharding import PartitionSpec as P

HEADS = 16
KV_HEADS = 8
HEAD_DIM = 64
EXPERTS = 32
EXP_FF = 512
TOP = 8
CAP = 108
CAP_PAD = 112


norm_eps = 1e-05
rope_theta = 10000.0
excluded = -1e30


def rms_inverse(values):
    return lax.rsqrt(jnp.mean(values * values, axis=-1, keepdims=True) + norm_eps)


def norm_back(grad_act, normed, inverse, gain_vec):
    scaled = grad_act * gain_vec
    gain_grad = jnp.sum(grad_act * normed, axis=0)
    return (
        inverse * (scaled - normed * jnp.mean(scaled * normed, axis=-1, keepdims=True)),
        gain_grad,
    )


def rope_tables(seq_len, head_size):
    half_size = head_size // 2
    exponent = jnp.arange(half_size, dtype=jnp.float32) * (2.0 / head_size)
    frequency = rope_theta ** (-exponent)
    angles = jnp.arange(seq_len, dtype=jnp.float32)[:, None] * frequency[None, :]
    return (jnp.cos(angles), jnp.sin(angles))


def rotate(values, cosine, sine_table):
    half_size = values.shape[-1] // 2
    front_part = values[..., :half_size]
    back_part = values[..., half_size:]
    cos_b = cosine[:, None, :]
    sin_b = sine_table[:, None, :]
    return jnp.concatenate(
        [front_part * cos_b - back_part * sin_b, back_part * cos_b + front_part * sin_b], axis=-1
    )


def allowed_mask(seq_len, picture):
    position = jnp.arange(seq_len, dtype=jnp.int32)
    causal = position[None, :] <= position[:, None]
    inside = (position >= picture[0]) & (position < picture[1])
    return causal | inside[:, None] & inside[None, :]


def slot_table(routes_seq, fill_rows):
    seq_len = fill_rows.shape[0]
    position = jnp.arange(seq_len, dtype=jnp.int32)
    member = jnp.any(
        routes_seq[:, :, None] == jnp.arange(EXPERTS, dtype=jnp.int32)[None, None, :], axis=1
    )
    rank = jnp.sum(
        jnp.where(fill_rows[None, :] == position[:, None], position[None, :], 0), axis=1
    )
    earlier = (rank[None, :] < rank[:, None]).astype(jnp.bfloat16)
    count = jnp.dot(
        earlier, member.astype(jnp.bfloat16), preferred_element_type=jnp.float32
    )
    return jnp.where(member, jnp.minimum(count, float(CAP)), -1.0)


def attention_scores(queries, key_rows, allowed, scale_factor):
    raw_scores = jnp.einsum("qkgd,skd->kgqs", queries, key_rows, preferred_element_type=jnp.float32)
    return jnp.where(allowed, raw_scores * scale_factor, excluded)


def gates_of(acts, router, slots):
    logits = jnp.einsum("...d,de->...e", acts, router, preferred_element_type=jnp.float32)
    member = slots >= 0
    top_value = jnp.max(jnp.where(member, logits, excluded), axis=-1, keepdims=True)
    powers = jnp.where(member, jnp.exp(logits - top_value), 0.0)
    return powers / jnp.sum(powers, axis=-1, keepdims=True)


def fold_order(count):
    return list(range(0, count, 2))[:1] + list(range(1, count, 2)) + list(range(2, count, 2))[::-1]


def pick(table, index):
    value = jnp.int32(table[0])
    for place, entry in enumerate(table[1:], 1):
        value = jnp.where(index == place, jnp.int32(entry), value)
    return value


def ring_of(axis, count):
    me = lax.axis_index(axis)
    half, side = me // 2, me % 2
    order = fold_order(count // 2)
    inverse = [order.index(place) for place in range(count // 2)]
    spot = pick(inverse, half)

    def behind(distance):
        return pick(order, lax.rem(spot - distance + count, count // 2))

    return side, behind


def nt_dot(left, right):
    return lax.dot_general(
        left, right, (((1,), (1,)), ((), ())), preferred_element_type=jnp.float32
    )


def tn_dot(left, right):
    return lax.dot_general(
        left, right, (((0,), (0,)), ((), ())), preferred_element_type=jnp.float32
    )


def plain_dot(left, right):
    return jnp.dot(left, right, preferred_element_type=jnp.float32)


def greet(axis, peers):
    barrier = pltpu.get_barrier_semaphore()
    for peer in peers:
        pl.semaphore_signal(
            barrier, inc=1, device_id={axis: peer}, device_id_type=pl.DeviceIdType.MESH
        )
    pl.semaphore_wait(barrier, len(peers))


def expert_kernel(
    count,
    act_ref,
    dy_ref,
    slot_ref,
    router_ref,
    wgu_ref,
    wdn_ref,
    mix_ref,
    back_ref,
    pair_ref,
    disp_ref,
    inner_ref,
    gug_ref,
    gb_ref,
    xbuf,
    dybuf,
    wgu,
    wdn,
    gates,
    hot_s,
    gate_s,
    disp_s,
    dyr_s,
    inner_s,
    fgate_s,
    fup_s,
    wt_s,
    gb_s,
    gug_s,
    in_s,
    out_s,
    w_sem,
    own_sem,
    dy_sem,
    ring_send,
    ring_recv,
    pair_send,
    pair_recv,
    save_sem,
    out_sem,
):
    local = wgu_ref.shape[0]
    rings = count // 2
    me = lax.axis_index("expert")
    side, behind = ring_of("expert", count)
    nxt = 2 * behind(rings - 1) + side
    prev = 2 * behind(1) + side
    mate = me + 1 - 2 * side
    first = me * local

    load_wgu = pltpu.make_async_copy(wgu_ref, wgu, w_sem.at[0])
    load_wdn = pltpu.make_async_copy(wdn_ref, wdn, w_sem.at[1])
    load_wgu.start()
    pair_ref[...] = jnp.zeros_like(pair_ref)
    load_wdn.start()
    own = pltpu.make_async_copy(act_ref, xbuf.at[0, 0], own_sem)
    own.start()

    def dy_copy(group, lane):
        sequence = 2 * behind(group) + jnp.where(lane == 0, side, 1 - side)
        return pltpu.make_async_copy(
            dy_ref.at[sequence], dybuf.at[lax.rem(group, 2), lane], dy_sem.at[lax.rem(group, 2), lane]
        )

    for lane in range(2):
        dy_copy(0, lane).start()
    own.wait()
    if rings > 2:
        greet("expert", (nxt, prev, mate))
    elif rings == 2:
        greet("expert", (nxt, mate))
    else:
        greet("expert", (mate,))

    def to_next(group):
        return pltpu.make_async_remote_copy(
            src_ref=xbuf.at[group, 0],
            dst_ref=xbuf.at[group + 1, 0],
            send_sem=ring_send.at[group],
            recv_sem=ring_recv.at[group + 1],
            device_id={"expert": nxt},
            device_id_type=pl.DeviceIdType.MESH,
        )

    def to_mate(group):
        return pltpu.make_async_remote_copy(
            src_ref=xbuf.at[group, 0],
            dst_ref=xbuf.at[group, 1],
            send_sem=pair_send.at[group],
            recv_sem=pair_recv.at[group],
            device_id={"expert": mate},
            device_id_type=pl.DeviceIdType.MESH,
        )

    if rings > 1:
        to_next(0).start()
    to_mate(0).start()
    load_wgu.wait()
    load_wdn.wait()

    def saves(group):
        rows = pl.ds(pl.multiple_of(group * 2 * CAP_PAD, 16), 2 * CAP_PAD)
        return [
            pltpu.make_async_copy(disp_s, disp_ref.at[:, rows], save_sem.at[0]),
            pltpu.make_async_copy(inner_s, inner_ref.at[:, rows], save_sem.at[1]),
            pltpu.make_async_copy(gug_s, gug_ref.at[:, rows], save_sem.at[2]),
            pltpu.make_async_copy(gb_s, gb_ref.at[:, rows], save_sem.at[3]),
        ]

    def outs(group, lane):
        sequence = 2 * behind(group) + jnp.where(lane == 0, side, 1 - side)
        return [
            pltpu.make_async_copy(out_s.at[lane, 0], mix_ref.at[sequence], out_sem.at[lane, 0]),
            pltpu.make_async_copy(out_s.at[lane, 1], back_ref.at[sequence], out_sem.at[lane, 1]),
        ]

    slot_iota = lax.broadcasted_iota(jnp.int32, (CAP_PAD, act_ref.shape[0]), 0).astype(jnp.float32)

    def compute(group):
        to_mate(group).wait_recv()
        parity = lax.rem(group, 2)

        @pl.when(group + 1 < rings)
        def _():
            for lane in range(2):
                dy_copy(group + 1, lane).start()

        for lane in range(2):
            dy_copy(group, lane).wait()

        @pl.when(group > 0)
        def _():
            for copy in saves(group - 1):
                copy.wait()

        for lane in range(2):
            sequence = 2 * behind(group) + (side if lane == 0 else 1 - side)
            acts = xbuf[group, lane]
            slots = slot_ref[sequence]
            logits = nt_dot(router_ref[...], acts)
            member = slots >= 0
            top_value = jnp.max(jnp.where(member, logits, excluded), axis=0, keepdims=True)
            powers = jnp.where(member, jnp.exp(logits - top_value), 0.0)
            gates[...] = powers / jnp.sum(powers, axis=0, keepdims=True)
            for e in range(local):
                slot = slot_ref[sequence, pl.ds(first + e, 1), :]
                gate = gates[pl.ds(first + e, 1), :]
                hot = (slot_iota == slot) & (slot < CAP)
                gate_s[e, lane * CAP_PAD : (lane + 1) * CAP_PAD, :] = jnp.sum(
                    jnp.where(hot, gate, 0.0), axis=1, keepdims=True
                )
                hot_s[lane, e * CAP_PAD : (e + 1) * CAP_PAD, :] = jnp.where(hot, 1.0, 0.0).astype(
                    jnp.bfloat16
                )
            rows = plain_dot(hot_s[lane], acts).astype(jnp.bfloat16)
            dy_rows = plain_dot(hot_s[lane], dybuf[parity, lane]).astype(jnp.bfloat16)
            for e in range(local):
                span = slice(lane * CAP_PAD, (lane + 1) * CAP_PAD)
                disp_s[e, span, :] = rows[e * CAP_PAD : (e + 1) * CAP_PAD]
                dyr_s[e, span, :] = dy_rows[e * CAP_PAD : (e + 1) * CAP_PAD]

        def one_expert(e, carry):
            width = act_ref.shape[1]
            ff = wdn.shape[1]
            step = 256
            for n in range(ff // step):
                cols = slice(n * step, (n + 1) * step)
                gate_part = plain_dot(disp_s[e], wgu[e, :, cols])
                up_part = plain_dot(disp_s[e], wgu[e, :, ff + n * step : ff + (n + 1) * step])
                sig = jax.nn.sigmoid(gate_part)
                fup = gate_part * sig
                fup_s[:, cols] = fup
                fgate_s[:, cols] = up_part * sig * (1.0 + gate_part * (1.0 - sig))
                inner_s[e, :, cols] = (fup * up_part).astype(jnp.bfloat16)
            gate_col = gate_s[e]
            pair_col = jnp.zeros_like(gate_col)
            for n in range(width // step):
                cols = slice(n * step, (n + 1) * step)
                made = plain_dot(inner_s[e], wdn[e, :, cols])
                dy_rows = dyr_s[e, :, cols].astype(jnp.float32)
                pair_col = pair_col + jnp.sum(made * dy_rows, axis=1, keepdims=True)
                weighted = (made * gate_col).astype(jnp.bfloat16)
                gb_s[e, :, cols] = (dy_rows * gate_col).astype(jnp.bfloat16)
                for lane in range(2):
                    wt_s[lane, e, :, cols] = weighted[lane * CAP_PAD : (lane + 1) * CAP_PAD]
            for lane in range(2):
                sequence = 2 * behind(group) + (side if lane == 0 else 1 - side)
                hot = hot_s[lane, pl.ds(pl.multiple_of(e * CAP_PAD, 16), CAP_PAD), :]
                pair_ref[sequence, pl.ds(first + e, 1), :] = jnp.sum(
                    hot.astype(jnp.float32) * pair_col[lane * CAP_PAD : (lane + 1) * CAP_PAD],
                    axis=0,
                    keepdims=True,
                )
            for n in range(ff // step):
                cols = slice(n * step, (n + 1) * step)
                grad = nt_dot(gb_s[e], wdn[e, cols, :])
                gug_s[e, :, cols] = (grad * fgate_s[:, cols]).astype(jnp.bfloat16)
                gug_s[e, :, ff + n * step : ff + (n + 1) * step] = (grad * fup_s[:, cols]).astype(
                    jnp.bfloat16
                )
            for n in range(width // step):
                cols = slice(n * step, (n + 1) * step)
                grad = nt_dot(gug_s[e], wgu[e, cols, :]).astype(jnp.bfloat16)
                for lane in range(2):
                    in_s[lane, e, :, cols] = grad[lane * CAP_PAD : (lane + 1) * CAP_PAD]
            return carry

        lax.fori_loop(0, local, one_expert, 0)
        for copy in saves(group):
            copy.start()
        for lane in range(2):

            @pl.when(group > 0)
            def _():
                for copy in outs(group - 1, lane):
                    copy.wait()

            width = act_ref.shape[1]
            flat = (local * CAP_PAD, width)
            out_s[lane, 0] = tn_dot(hot_s[lane], wt_s[lane].reshape(flat)).astype(jnp.bfloat16)
            out_s[lane, 1] = tn_dot(hot_s[lane], in_s[lane].reshape(flat)).astype(jnp.bfloat16)
            for copy in outs(group, lane):
                copy.start()

    def step(group, carry):
        to_next(group - 1).wait_recv()

        @pl.when(group + 1 < rings)
        def _():
            to_next(group).start()

        to_mate(group).start()
        compute(group - 1)
        return carry

    lax.fori_loop(1, rings, step, 0)
    compute(rings - 1)
    for copy in saves(rings - 1) + outs(rings - 1, 0) + outs(rings - 1, 1):
        copy.wait()

    def drain(group, carry):
        to_mate(group).wait_send()

        @pl.when(group + 1 < rings)
        def _():
            to_next(group).wait_send()

        return carry

    lax.fori_loop(0, rings, drain, 0)


def expert_stage(act_two, grads_all, slots_all, router_t, w_gate_up, w_down):
    count, seq_len, width = grads_all.shape
    local, _, wide = w_gate_up.shape
    ff = w_down.shape[1]
    rows = count * CAP_PAD
    group_rows = 2 * CAP_PAD
    bf, f32 = jnp.bfloat16, jnp.float32
    anywhere = pl.BlockSpec(memory_space=pl.ANY)
    vmem = pl.BlockSpec(memory_space=pltpu.VMEM)
    flops = 2 * rows * local * width * ff * 6 + 8 * count * local * CAP_PAD * seq_len * width
    return pl.pallas_call(
        functools.partial(expert_kernel, count),
        out_shape=(
            jax.ShapeDtypeStruct((count, seq_len, width), bf),
            jax.ShapeDtypeStruct((count, seq_len, width), bf),
            jax.ShapeDtypeStruct((count, EXPERTS, seq_len), f32),
            jax.ShapeDtypeStruct((local, rows, width), bf),
            jax.ShapeDtypeStruct((local, rows, ff), bf),
            jax.ShapeDtypeStruct((local, rows, wide), bf),
            jax.ShapeDtypeStruct((local, rows, width), bf),
        ),
        in_specs=[anywhere, anywhere, vmem, vmem, anywhere, anywhere],
        out_specs=(anywhere, anywhere, vmem, anywhere, anywhere, anywhere, anywhere),
        scratch_shapes=[
            pltpu.VMEM((count // 2, 2, seq_len, width), bf),
            pltpu.VMEM((2, 2, seq_len, width), bf),
            pltpu.VMEM((local, width, wide), bf),
            pltpu.VMEM((local, ff, width), bf),
            pltpu.VMEM((EXPERTS, seq_len), f32),
            pltpu.VMEM((2, local * CAP_PAD, seq_len), bf),
            pltpu.VMEM((local, group_rows, 1), f32),
            pltpu.VMEM((local, group_rows, width), bf),
            pltpu.VMEM((local, group_rows, width), bf),
            pltpu.VMEM((local, group_rows, ff), bf),
            pltpu.VMEM((group_rows, ff), f32),
            pltpu.VMEM((group_rows, ff), f32),
            pltpu.VMEM((2, local, CAP_PAD, width), bf),
            pltpu.VMEM((local, group_rows, width), bf),
            pltpu.VMEM((local, group_rows, wide), bf),
            pltpu.VMEM((2, local, CAP_PAD, width), bf),
            pltpu.VMEM((2, 2, seq_len, width), bf),
            pltpu.SemaphoreType.DMA((2,)),
            pltpu.SemaphoreType.DMA,
            pltpu.SemaphoreType.DMA((2, 2)),
            pltpu.SemaphoreType.DMA((count // 2,)),
            pltpu.SemaphoreType.DMA((count // 2,)),
            pltpu.SemaphoreType.DMA((count // 2,)),
            pltpu.SemaphoreType.DMA((count // 2,)),
            pltpu.SemaphoreType.DMA((4,)),
            pltpu.SemaphoreType.DMA((2, 2)),
        ],
        compiler_params=pltpu.CompilerParams(
            collective_id=0, has_side_effects=True, vmem_limit_bytes=60 << 20
        ),
        cost_estimate=pl.CostEstimate(
            flops=flops, bytes_accessed=60 << 20, transcendentals=rows * local * ff
        ),
        name="expert_stage",
    )(act_two, grads_all, slots_all, router_t, w_gate_up, w_down)


def send(src, dst, send_sem, recv_sem, axis, peer):
    return pltpu.make_async_remote_copy(
        src_ref=src,
        dst_ref=dst,
        send_sem=send_sem,
        recv_sem=recv_sem,
        device_id={axis: peer},
        device_id_type=pl.DeviceIdType.MESH,
    )


def neighbours(axis, count):
    rings = count // 2
    side, behind = ring_of(axis, count)
    me = lax.axis_index(axis)
    mate = me + 1 - 2 * side
    nxt = 2 * behind(rings - 1) + side
    prev = 2 * behind(1) + side
    peers = [mate] + ([nxt] if rings > 1 else []) + ([prev] if rings > 2 else [])
    return side, behind, mate, nxt, peers


def greet_all(peers_of):
    barrier = pltpu.get_barrier_semaphore()
    for axis, peers in peers_of:
        for peer in peers:
            pl.semaphore_signal(
                barrier, inc=1, device_id={axis: peer}, device_id_type=pl.DeviceIdType.MESH
            )
    pl.semaphore_wait(barrier, sum(len(peers) for _, peers in peers_of))


class ScatterSum:
    def scratch(count, block, kind):
        rings = count // 2
        deep = min(2, rings)
        return [
            pltpu.VMEM((rings,) + block, kind),
            pltpu.VMEM((rings,) + block, kind),
            pltpu.VMEM((deep,) + block, kind),
            pltpu.VMEM((deep,) + block, kind),
            pltpu.SemaphoreType.DMA((rings,)),
            pltpu.SemaphoreType.DMA((rings,)),
            pltpu.SemaphoreType.DMA((rings,)),
            pltpu.SemaphoreType.DMA((rings,)),
            pltpu.SemaphoreType.DMA((deep,)),
        ]

    def __init__(self, axis, count, part_ref, refs):
        self.axis, self.count, self.part = axis, count, part_ref
        self.rings = count // 2
        self.order = list(range(1, self.rings)) + [0]
        self.side, self.behind, self.mate, self.nxt, _ = neighbours(axis, count)
        (
            self.pair,
            self.ring,
            self.own,
            self.out,
            self.pair_send,
            self.pair_recv,
            self.ring_send,
            self.ring_recv,
            self.own_sem,
        ) = refs

    def to_mate(self, k):
        return send(
            self.part.at[2 * self.behind(k) + 1 - self.side],
            self.pair.at[k],
            self.pair_send.at[k],
            self.pair_recv.at[k],
            self.axis,
            self.mate,
        )

    def to_next(self, k):
        place = (k + 1) % self.rings
        return send(
            self.out.at[k % self.out.shape[0]],
            self.ring.at[place],
            self.ring_send.at[k],
            self.ring_recv.at[place],
            self.axis,
            self.nxt,
        )

    def load(self, at):
        k = self.order[at]
        slot = at % self.own.shape[0]
        return pltpu.make_async_copy(
            self.part.at[2 * self.behind(k) + self.side], self.own.at[slot], self.own_sem.at[slot]
        )

    def begin_load(self):
        for at in range(min(self.own.shape[0], self.rings)):
            self.load(at).start()

    def begin(self):
        for k in self.order:
            self.to_mate(k).start()

    def step(self, at, store=None):
        k = self.order[at]
        slot = at % self.own.shape[0]
        self.load(at).wait()
        self.to_mate(k).wait_recv()
        if at > 0:
            self.to_next((k - 1) % self.rings).wait_recv()
        deep = self.out.shape[0]
        if k >= 1 and k - deep >= 1:
            self.to_next(k - deep).wait_send()
        rows = self.own.shape[1]
        piece = 128 if rows % 128 == 0 and len(self.own.shape) == 3 else rows
        for start in range(0, rows, piece):
            span = slice(start, start + piece)
            value = self.own[slot, span].astype(jnp.float32) + self.pair[k, span].astype(jnp.float32)
            if at > 0:
                value = value + self.ring[k, span].astype(jnp.float32)
            if k == 0:
                store(span, value)
            else:
                self.out[k % deep, span] = value.astype(self.out.dtype)
        if k > 0:
            self.to_next(k).start()
        if at + self.own.shape[0] < self.rings:
            self.load(at + self.own.shape[0]).start()

    def finish(self):
        deep = self.out.shape[0]
        for k in range(max(1, self.rings - deep), self.rings):
            self.to_next(k).wait_send()
        for k in self.order:
            self.to_mate(k).wait_send()


class WholeSum:
    def scratch(count, rows, width):
        rings = count // 2
        steps = max(rings - 1, 1)
        block = (rows, width)
        return [
            pltpu.VMEM((rings,) + block, jnp.bfloat16),
            pltpu.VMEM((steps,) + block, jnp.bfloat16),
            pltpu.VMEM((rings,) + block, jnp.bfloat16),
            pltpu.VMEM((rings,) + block, jnp.bfloat16),
            pltpu.SemaphoreType.DMA((2,)),
            pltpu.SemaphoreType.DMA((steps,)),
            pltpu.SemaphoreType.DMA((steps,)),
            pltpu.SemaphoreType.DMA((steps,)),
            pltpu.SemaphoreType.DMA((rings,)),
            pltpu.SemaphoreType.DMA((rings,)),
            pltpu.SemaphoreType.DMA((rings,)),
        ]

    def __init__(self, axis, count, gw, refs):
        self.axis, self.count, self.gw = axis, count, gw
        self.rings = count // 2
        self.side, self.behind, self.mate, self.nxt, _ = neighbours(axis, count)
        (
            self.got,
            self.ring,
            self.full,
            self.other,
            self.swap_sem,
            self.ring_send,
            self.ring_recv,
            self.back_send,
            self.back_recv,
            self.give_send,
            self.give_recv,
        ) = refs

    def swap(self):
        return send(
            self.gw.at[1 - self.side], self.got, self.swap_sem.at[0], self.swap_sem.at[1], self.axis, self.mate
        )

    def to_next(self, k):
        return send(
            self.got.at[self.behind(k)],
            self.ring.at[k - 1],
            self.ring_send.at[k - 1],
            self.ring_recv.at[k - 1],
            self.axis,
            self.nxt,
        )

    def back(self, g):
        return send(
            self.full.at[g],
            self.full.at[g + 1],
            self.back_send.at[g],
            self.back_recv.at[g + 1],
            self.axis,
            self.nxt,
        )

    def give(self, g):
        return send(
            self.full.at[g], self.other.at[g], self.give_send.at[g], self.give_recv.at[g], self.axis, self.mate
        )

    def begin(self):
        self.swap().start()

    def pair_done(self):
        self.swap().wait_recv()
        for part in range(self.rings):
            total = self.gw[self.side, part].astype(jnp.float32) + self.got[part].astype(jnp.float32)
            self.got[part] = total.astype(jnp.bfloat16)
        if self.rings > 1:
            self.to_next(1).start()

    def ring_done(self):
        for k in range(2, self.rings):
            self.to_next(k - 1).wait_recv()
            part = self.behind(k)
            total = self.got[part].astype(jnp.float32) + self.ring[k - 2].astype(jnp.float32)
            self.got[part] = total.astype(jnp.bfloat16)
            self.to_next(k).start()
        part = self.behind(0)
        total = self.got[part].astype(jnp.float32)
        if self.rings > 1:
            self.to_next(self.rings - 1).wait_recv()
            total = total + self.ring[self.rings - 2].astype(jnp.float32)
        self.full[0] = total.astype(jnp.bfloat16)
        if self.rings > 1:
            self.back(0).start()
        self.give(0).start()

    def back_done(self):
        for g in range(1, self.rings):
            self.back(g - 1).wait_recv()
            if g + 1 < self.rings:
                self.back(g).start()
            self.give(g).start()

    def finish(self):
        self.swap().wait_send()
        for k in range(1, self.rings):
            self.to_next(k).wait_send()
        for g in range(self.rings):
            if g + 1 < self.rings:
                self.back(g).wait_send()
            self.give(g).wait_send()


class Gather:
    def scratch(count):
        rings = count // 2
        return [pltpu.SemaphoreType.DMA((rings,)) for _ in range(4)] + [pltpu.SemaphoreType.DMA]

    def __init__(self, axis, count, own_ref, out_ref, refs):
        self.axis, self.count, self.own, self.out = axis, count, own_ref, out_ref
        self.rings = count // 2
        self.side, self.behind, self.mate, self.nxt, _ = neighbours(axis, count)
        self.ring_send, self.ring_recv, self.pair_send, self.pair_recv, self.own_sem = refs

    def block(self, g):
        return self.own if g == 0 else self.out.at[2 * self.behind(g) + self.side]

    def to_next(self, g):
        return send(
            self.block(g),
            self.out.at[2 * self.behind(g) + self.side],
            self.ring_send.at[g],
            self.ring_recv.at[g + 1],
            self.axis,
            self.nxt,
        )

    def to_mate(self, g):
        return send(
            self.block(g),
            self.out.at[2 * self.behind(g) + self.side],
            self.pair_send.at[g],
            self.pair_recv.at[g],
            self.axis,
            self.mate,
        )

    def keep_own(self):
        return pltpu.make_async_copy(
            self.own, self.out.at[2 * self.behind(0) + self.side], self.own_sem
        )

    def begin(self):
        if self.rings > 1:
            self.to_next(0).start()
        self.to_mate(0).start()
        self.keep_own().start()

    def step(self, g):
        self.to_next(g - 1).wait_recv()
        if g + 1 < self.rings:
            self.to_next(g).start()
        self.to_mate(g).start()

    def finish(self):
        self.keep_own().wait()
        for g in range(self.rings):
            self.to_mate(g).wait_recv()
        for g in range(self.rings):
            self.to_mate(g).wait_send()
            if g + 1 < self.rings:
                self.to_next(g).wait_send()


def weights_kernel(dp_count, count, number, *refs):
    ins, outs, rest = refs[: number + 1], refs[number + 1 : 2 * number + 2], list(refs[2 * number + 2 :])
    gathers = []
    for at in range(number + 1):
        axis, size = ("dp", dp_count) if at < number else ("expert", count)
        gathers.append(Gather(axis, size, ins[at], outs[at], rest[:5]))
        rest = rest[5:]
    greet_all([("dp", neighbours("dp", dp_count)[4]), ("expert", neighbours("expert", count)[4])])
    for gather in gathers:
        gather.begin()
    for g in range(1, max(dp_count, count) // 2):
        for gather in gathers:
            if g < gather.rings:
                gather.step(g)
    for gather in gathers:
        gather.finish()


def weights_stage(blocks, slots, dp_count, count):
    number = len(blocks)
    sizes = [dp_count] * number + [count]
    vmem = pl.BlockSpec(memory_space=pltpu.VMEM)
    anywhere = pl.BlockSpec(memory_space=pl.ANY)
    return pl.pallas_call(
        functools.partial(weights_kernel, dp_count, count, number),
        out_shape=tuple(
            jax.ShapeDtypeStruct((size,) + block.shape, block.dtype)
            for size, block in zip(sizes, list(blocks) + [slots])
        ),
        in_specs=[vmem] * (number + 1),
        out_specs=(anywhere,) * (number + 1),
        scratch_shapes=[ref for size in sizes for ref in Gather.scratch(size)],
        compiler_params=pltpu.CompilerParams(
            collective_id=2, has_side_effects=True, vmem_limit_bytes=16 << 20
        ),
        cost_estimate=pl.CostEstimate(flops=0, bytes_accessed=100 << 20, transcendentals=0),
        name="weights_stage",
    )(*blocks, slots)


def emit_sum(whole, out_ref, sem):
    copies = []
    for g in range(whole.rings):
        part = whole.behind(g)
        copies.append(
            pltpu.make_async_copy(whole.full.at[g], out_ref.at[whole.side, part], sem.at[0, g])
        )
        copies.append(
            pltpu.make_async_copy(whole.other.at[g], out_ref.at[1 - whole.side, part], sem.at[1, g])
        )
    return copies


def scatter_kernel(count, dp_count, sizes, *refs):
    back_ref, pair_ref, disp_ref, inner_ref, gug_ref, gb_ref = refs[:6]
    back_out, pair_out, sum_out, raw_out = refs[6:10]
    rest = list(refs[10:])

    def take(number):
        got, rest[:] = rest[:number], rest[number:]
        return got

    local, early, chunks, chunk, width, ff = sizes
    parts = dp_count // 2
    up_rows, down_rows = width // (2 * parts), ff // (2 * parts)
    back = ScatterSum("expert", count, back_ref, take(9))
    pair = ScatterSum("expert", count, pair_ref, take(9))
    gw_all, load_bufs, load_sem = take(1)[0], take(4), take(1)[0]
    total = take(1)[0] if chunks > 1 else None
    whole = [WholeSum("dp", dp_count, gw_all.at[e], take(11)) for e in range(early)]
    emit_sem, raw_sem = take(2)

    def loads(e, piece, slot):
        rows = pl.ds(pl.multiple_of(piece * chunk, 16), chunk)
        return [
            pltpu.make_async_copy(ref.at[e, rows], buf.at[slot], load_sem.at[slot, i])
            for i, (ref, buf) in enumerate(zip((disp_ref, inner_ref, gug_ref, gb_ref), load_bufs))
        ]

    def weights(e):
        disp, inner, gug, gb = load_bufs

        def products(slot, use):
            for half in range(2):
                for part in range(parts):
                    up_at = (half * parts + part) * up_rows
                    down_at = (half * parts + part) * down_rows
                    use(
                        half,
                        part,
                        tn_dot(disp[slot, :, up_at : up_at + up_rows], gug[slot]),
                        tn_dot(inner[slot, :, down_at : down_at + down_rows], gb[slot]),
                    )

        def keep(half, part, up, down):
            gw_all[e, half, part, :up_rows] = up.astype(jnp.bfloat16)
            gw_all[e, half, part, up_rows:] = down.astype(jnp.bfloat16)

        def gather(half, part, up, down):
            total[half, part, :up_rows] += up
            total[half, part, up_rows:] += down

        if chunks == 1:
            for copy in loads(e, 0, e % 2):
                copy.wait()
            products(e % 2, keep)
            if e + 2 < local:
                for copy in loads(e + 2, 0, e % 2):
                    copy.start()
        else:
            total[...] = jnp.zeros_like(total)

            def one(piece, carry):
                for copy in loads(e, piece, 0):
                    copy.start()
                for copy in loads(e, piece, 0):
                    copy.wait()
                products(0, gather)
                return carry

            lax.fori_loop(0, chunks, one, 0)
            for half in range(2):
                for part in range(parts):
                    gw_all[e, half, part] = total[half, part].astype(jnp.bfloat16)

    def keep_back(span, value):
        back_out[span] = value

    def keep_pair(span, value):
        pair_out[span] = value

    def raw(e):
        return pltpu.make_async_copy(gw_all.at[e], raw_out.at[e - early], raw_sem.at[e - early])

    if chunks == 1:
        for e in range(min(2, local)):
            for copy in loads(e, 0, e):
                copy.start()
    back.begin_load()
    pair.begin_load()
    greet_all([("expert", neighbours("expert", count)[4]), ("dp", neighbours("dp", dp_count)[4])])
    back.begin()
    pair.begin()
    steps = count // 2
    made = 0

    def make(stop):
        nonlocal made
        while made < min(stop, local):
            weights(made)
            if made < early:
                whole[made].begin()
            else:
                raw(made).start()
            made += 1

    make(1)
    make(2)
    whole[0].pair_done()
    for turn in range(steps):
        back.step(turn, keep_back)
        pair.step(turn, keep_pair)
        make(turn + 3)
        if turn + 1 < early:
            whole[turn + 1].pair_done()
        if turn == steps // 2:
            whole[0].ring_done()
    make(local)
    for e in range(steps + 1, early):
        whole[e].pair_done()
    for e in range(1, early):
        whole[e].ring_done()
    for e in range(early):
        whole[e].back_done()
    for e in range(early):
        for g in range(parts):
            whole[e].give(g).wait_recv()
        for copy in emit_sum(whole[e], sum_out.at[e], emit_sem.at[e]):
            copy.start()
    for e in range(early):
        for copy in emit_sum(whole[e], sum_out.at[e], emit_sem.at[e]):
            copy.wait()
    for e in range(early, local):
        raw(e).wait()
    back.finish()
    pair.finish()
    for e in range(early):
        whole[e].finish()


def scatter_stage(back_part, pair_part, disp, inner, gug, gb, dp_count, early):
    count, seq_len, width = back_part.shape
    local, rows, ff = inner.shape
    wide = gug.shape[2]
    bf, f32 = jnp.bfloat16, jnp.float32
    chunk = rows if rows <= 8 * CAP_PAD else 4 * CAP_PAD
    chunks = rows // chunk
    parts = dp_count // 2
    part_rows = (width + ff) // (2 * parts)
    late = max(local - early, 1)
    anywhere = pl.BlockSpec(memory_space=pl.ANY)
    vmem = pl.BlockSpec(memory_space=pltpu.VMEM)
    scratch = (
        ScatterSum.scratch(count, (seq_len, width), bf)
        + ScatterSum.scratch(count, pair_part.shape[1:], f32)
        + [
            pltpu.VMEM((local, 2, parts, part_rows, width), bf),
            pltpu.VMEM((2, chunk, width), bf),
            pltpu.VMEM((2, chunk, ff), bf),
            pltpu.VMEM((2, chunk, wide), bf),
            pltpu.VMEM((2, chunk, width), bf),
            pltpu.SemaphoreType.DMA((2, 4)),
        ]
        + ([pltpu.VMEM((2, parts, part_rows, width), f32)] if chunks > 1 else [])
        + [ref for _ in range(early) for ref in WholeSum.scratch(dp_count, part_rows, width)]
        + [pltpu.SemaphoreType.DMA((early, 2, parts)), pltpu.SemaphoreType.DMA((late,))]
    )
    return pl.pallas_call(
        functools.partial(
            scatter_kernel, count, dp_count, (local, early, chunks, chunk, width, ff)
        ),
        out_shape=(
            jax.ShapeDtypeStruct((seq_len, width), f32),
            jax.ShapeDtypeStruct(pair_part.shape[1:], f32),
            jax.ShapeDtypeStruct((early, 2, parts, part_rows, width), bf),
            jax.ShapeDtypeStruct((late, 2, parts, part_rows, width), bf),
        ),
        in_specs=[anywhere] * 6,
        out_specs=(vmem, vmem, anywhere, anywhere),
        scratch_shapes=scratch,
        compiler_params=pltpu.CompilerParams(
            collective_id=1, has_side_effects=True, vmem_limit_bytes=63 << 20
        ),
        cost_estimate=pl.CostEstimate(
            flops=6 * local * rows * width * ff, bytes_accessed=200 << 20, transcendentals=0
        ),
        name="scatter_stage",
    )(back_part, pair_part, disp, inner, gug, gb)


def shared_kernel(count, dp_count, late, number, *refs):
    grads, raw_ref = refs[:number], refs[number]
    outs, sum_out = refs[number + 1 : 2 * number + 1], refs[2 * number + 1]
    rest = list(refs[2 * number + 2 :])

    def take(amount):
        got, rest[:] = rest[:amount], rest[amount:]
        return got

    firsts, seconds, thirds, mids, fulls = [], [], [], [], []
    for grad in grads:
        mid, own, full = take(3)
        mids.append(mid)
        firsts.append(ScatterSum("dp", dp_count, grad, take(9)))
        seconds.append(ScatterSum("expert", count, mid, take(9)))
        thirds.append((own, Gather("expert", count, own, full, take(5))))
        fulls.append(full)
    whole = []
    if late:
        gw, gw_sem, emit_sem = take(3)
        load = pltpu.make_async_copy(raw_ref, gw, gw_sem)
        load.start()
        whole = [WholeSum("dp", dp_count, gw.at[e], take(11)) for e in range(late)]
    for first in firsts:
        first.begin_load()
    greet_all([("expert", neighbours("expert", count)[4]), ("dp", neighbours("dp", dp_count)[4])])
    for first in firsts:
        first.begin()
    if late:
        load.wait()
    for each in whole:
        each.begin()

    def keep(ref):
        def store(span, value):
            ref[span] = value.astype(ref.dtype)

        return store

    steps, dp_steps = count // 2, dp_count // 2
    for turn in range(dp_steps):
        for first, mid in zip(firsts, mids):
            first.step(turn, keep(mid))
        if turn == 0:
            for each in whole:
                each.pair_done()
    for second in seconds:
        second.begin_load()
        second.begin()
    for turn in range(steps):
        for second, (own, third) in zip(seconds, thirds):
            second.step(turn, keep(own))
        if turn < len(whole):
            whole[turn].ring_done()
    for own, third in thirds:
        third.begin()
    for each in whole[steps:]:
        each.ring_done()
    for g in range(1, steps):
        for own, third in thirds:
            third.step(g)
    for (own, third), full, out in zip(thirds, fulls, outs):
        third.finish()
        out[...] = full[...].astype(jnp.float32)
    for each in whole:
        each.back_done()
    for e, each in enumerate(whole):
        for g in range(each.rings):
            each.give(g).wait_recv()
        for copy in emit_sum(each, sum_out.at[e], emit_sem.at[e]):
            copy.start()
    for e, each in enumerate(whole):
        for copy in emit_sum(each, sum_out.at[e], emit_sem.at[e]):
            copy.wait()
    for each in firsts + seconds + whole:
        each.finish()


def shared_stage(grads, raw, late, count, dp_count):
    bf, f32 = jnp.bfloat16, jnp.float32
    anywhere = pl.BlockSpec(memory_space=pl.ANY)
    vmem = pl.BlockSpec(memory_space=pltpu.VMEM)
    scratch = []
    for grad in grads:
        block = grad.shape[1:]
        scratch += [pltpu.VMEM(block, bf), pltpu.VMEM(block[1:], bf), pltpu.VMEM(block, bf)]
        scratch += ScatterSum.scratch(dp_count, block, bf)
        scratch += ScatterSum.scratch(count, block[1:], bf)
        scratch += Gather.scratch(count)
    if late:
        parts, part_rows, width = raw.shape[2:]
        scratch += [
            pltpu.VMEM(raw.shape, bf),
            pltpu.SemaphoreType.DMA,
            pltpu.SemaphoreType.DMA((late, 2, parts)),
        ]
        scratch += [ref for _ in range(late) for ref in WholeSum.scratch(dp_count, part_rows, width)]
    return pl.pallas_call(
        functools.partial(shared_kernel, count, dp_count, late, len(grads)),
        out_shape=tuple(jax.ShapeDtypeStruct(grad.shape[1:], f32) for grad in grads)
        + (jax.ShapeDtypeStruct(raw.shape, bf),),
        in_specs=[anywhere] * (len(grads) + 1),
        out_specs=(vmem,) * len(grads) + (anywhere,),
        scratch_shapes=scratch,
        compiler_params=pltpu.CompilerParams(
            collective_id=3, has_side_effects=True, vmem_limit_bytes=60 << 20
        ),
        cost_estimate=pl.CostEstimate(flops=0, bytes_accessed=200 << 20, transcendentals=0),
        name="shared_stage",
    )(*grads, raw)


def shards(
    tokens,
    cotangent,
    routes,
    fill_order,
    picture_span,
    w_query,
    w_keyval,
    w_output,
    w_router,
    gain_attn,
    gain_moe,
    w_gate_up,
    w_down,
):
    seq_len, width_model = tokens.shape
    dp_count, count = lax.axis_size("dp"), lax.axis_size("expert")
    small = jnp.concatenate(
        [
            w_router,
            gain_attn[:, None],
            gain_moe[:, None],
            jnp.zeros((w_router.shape[0], 128 - EXPERTS - 2), w_router.dtype),
        ],
        axis=1,
    )
    slots_own = slot_table(routes, fill_order[0])
    small_all, keyval_all, query_all, output_all, slots_all = weights_stage(
        (small, w_keyval, w_query, w_output), slots_own.T, dp_count, count
    )
    small_all, keyval_all, query_all, output_all = (
        each.reshape(-1, each.shape[-1]) for each in (small_all, keyval_all, query_all, output_all)
    )
    router_all = small_all[:, :EXPERTS]
    gain_one = small_all[:, EXPERTS]
    gain_two = small_all[:, EXPERTS + 1]
    grads_all = lax.all_gather(cotangent, "expert", axis=0)
    group_size = HEADS // KV_HEADS
    kv_cols = KV_HEADS * HEAD_DIM
    scale_factor = 1.0 / math.sqrt(HEAD_DIM)
    inputs = tokens.astype(jnp.float32)
    inverse_one = rms_inverse(inputs)
    normed_one = inputs * inverse_one
    gain_one_f = gain_one.astype(jnp.float32)
    act_one = (normed_one * gain_one_f).astype(jnp.bfloat16)
    query_lin = jnp.dot(act_one, query_all, preferred_element_type=jnp.float32)
    keyval_lin = jnp.dot(act_one, keyval_all, preferred_element_type=jnp.float32)
    cosine, sine_table = rope_tables(seq_len, HEAD_DIM)
    queries = rotate(query_lin.reshape(seq_len, HEADS, HEAD_DIM), cosine, sine_table).astype(
        jnp.bfloat16
    )
    queries = queries.reshape(seq_len, KV_HEADS, group_size, HEAD_DIM)
    key_rows = rotate(
        keyval_lin[:, :kv_cols].reshape(seq_len, KV_HEADS, HEAD_DIM), cosine, sine_table
    ).astype(jnp.bfloat16)
    values = keyval_lin[:, kv_cols:].reshape(seq_len, KV_HEADS, HEAD_DIM).astype(jnp.bfloat16)
    allowed = allowed_mask(seq_len, picture_span[0])
    scores = attention_scores(queries, key_rows, allowed, scale_factor)
    row_max = jnp.max(scores, axis=-1, keepdims=True)
    powers = jnp.exp(scores - row_max)
    row_total = jnp.sum(powers, axis=-1, keepdims=True)
    attention = powers / row_total
    log_total = row_max + jnp.log(row_total)
    attended = jnp.einsum(
        "kgqs,skd->qkgd", attention.astype(jnp.bfloat16), values, preferred_element_type=jnp.float32
    )
    attended = attended.reshape(seq_len, HEADS * HEAD_DIM).astype(jnp.bfloat16)
    hidden = inputs + jnp.dot(attended, output_all, preferred_element_type=jnp.float32)
    inverse_two = rms_inverse(hidden)
    normed_two = hidden * inverse_two
    gain_two_f = gain_two.astype(jnp.float32)
    act_two = (normed_two * gain_two_f).astype(jnp.bfloat16)
    mixture_part, back_part, pair_part, disp, inner, gug, gb = expert_stage(
        act_two, grads_all, slots_all, router_all.T, w_gate_up, w_down
    )
    local = w_gate_up.shape[0]
    early = max(local // 2, 1)
    late = local - early
    back, pair_grad, early_sum, raw = scatter_stage(
        back_part, pair_part, disp, inner, gug, gb, dp_count, early
    )
    pair_grad = pair_grad.T
    mixture_part, back = lax.optimization_barrier((mixture_part, back))
    mixture = lax.psum_scatter(
        mixture_part, "expert", scatter_dimension=0, tiled=False
    ).astype(jnp.float32)
    output = (hidden + mixture).astype(jnp.bfloat16)
    gate_own = gates_of(act_two, router_all, slots_own)
    grad_out = cotangent.astype(jnp.float32)
    logit_grad = (
        gate_own * (pair_grad - jnp.sum(gate_own * pair_grad, axis=1, keepdims=True))
    ).astype(jnp.bfloat16)
    act_two_grad = back + jnp.dot(logit_grad, router_all.T, preferred_element_type=jnp.float32)
    grad_router = jnp.dot(act_two.T, logit_grad, preferred_element_type=jnp.float32)
    norm_grad_two, grad_gain_two = norm_back(act_two_grad, normed_two, inverse_two, gain_two_f)
    hidden_grad = grad_out + norm_grad_two
    attn_grad = hidden_grad.astype(jnp.bfloat16)
    grad_output_w = jnp.dot(attended.T, attn_grad, preferred_element_type=jnp.float32)
    attended_grad = jnp.dot(attn_grad, output_all.T, preferred_element_type=jnp.float32).astype(
        jnp.bfloat16
    )
    attended_grad = attended_grad.reshape(seq_len, KV_HEADS, group_size, HEAD_DIM)
    scores_again = attention_scores(queries, key_rows, allowed, scale_factor)
    attention_again = jnp.exp(scores_again - log_total)
    prob_grad = jnp.einsum(
        "qkgd,skd->kgqs", attended_grad, values, preferred_element_type=jnp.float32
    )
    row_dot = jnp.sum(attention_again * prob_grad, axis=-1, keepdims=True)
    score_grad = (attention_again * (prob_grad - row_dot) * scale_factor).astype(jnp.bfloat16)
    query_grad = jnp.einsum(
        "kgqs,skd->qkgd", score_grad, key_rows, preferred_element_type=jnp.float32
    )
    key_grad = jnp.einsum("kgqs,qkgd->skd", score_grad, queries, preferred_element_type=jnp.float32)
    value_grad = jnp.einsum(
        "kgqs,qkgd->skd",
        attention_again.astype(jnp.bfloat16),
        attended_grad,
        preferred_element_type=jnp.float32,
    )
    query_lin_grad = rotate(query_grad.reshape(seq_len, HEADS, HEAD_DIM), cosine, -sine_table)
    query_lin_grad = query_lin_grad.reshape(seq_len, HEADS * HEAD_DIM).astype(jnp.bfloat16)
    key_lin_grad = rotate(key_grad, cosine, -sine_table).reshape(seq_len, kv_cols)
    keyval_lin_grad = jnp.concatenate(
        [key_lin_grad, value_grad.reshape(seq_len, kv_cols)], axis=1
    ).astype(jnp.bfloat16)
    grad_query = jnp.dot(act_one.T, query_lin_grad, preferred_element_type=jnp.float32)
    grad_keyval = jnp.dot(act_one.T, keyval_lin_grad, preferred_element_type=jnp.float32)
    act_one_grad = jnp.dot(query_lin_grad, query_all.T, preferred_element_type=jnp.float32)
    act_one_grad = act_one_grad + jnp.dot(
        keyval_lin_grad, keyval_all.T, preferred_element_type=jnp.float32
    )
    norm_grad_one, grad_gain_one = norm_back(act_one_grad, normed_one, inverse_one, gain_one_f)
    grad_tokens = hidden_grad + norm_grad_one
    small_grad = jnp.concatenate(
        [
            grad_router,
            grad_gain_one[:, None],
            grad_gain_two[:, None],
            jnp.zeros((width_model, 128 - EXPERTS - 2), jnp.float32),
        ],
        axis=1,
    )
    blocks = [
        each.astype(jnp.bfloat16).reshape(dp_count, count, -1, each.shape[1])
        for each in (grad_output_w, grad_keyval, grad_query, small_grad)
    ]
    sum_output, sum_keyval, sum_query, sum_small, late_sum = shared_stage(
        blocks, raw, late, count, dp_count
    )
    sum_output, sum_keyval, sum_query, sum_small = (
        each.reshape(-1, each.shape[-1]) for each in (sum_output, sum_keyval, sum_query, sum_small)
    )
    sums = jnp.concatenate([early_sum, late_sum], axis=0) if late else early_sum
    up_rows = width_model // dp_count
    return (
        output,
        grad_tokens,
        sum_query,
        sum_keyval,
        sum_output,
        sum_small[:, :EXPERTS],
        sum_small[:, EXPERTS],
        sum_small[:, EXPERTS + 1],
        sums[:, :, :, :up_rows].astype(jnp.float32).reshape(w_gate_up.shape),
        sums[:, :, :, up_rows:].astype(jnp.float32).reshape(w_down.shape),
    )


def solution(mesh):
    return jax.shard_map(
        shards,
        mesh=mesh,
        in_specs=(
            P(("dp", "expert"), None),
            P(("dp", "expert"), None),
            P(("dp", "expert"), None),
            P(("dp", "expert"), None),
            P(("dp", "expert"), None),
            P("dp", None),
            P("dp", None),
            P("dp", None),
            P("dp", None),
            P("dp"),
            P("dp"),
            P("expert", None, None),
            P("expert", None, None),
        ),
        out_specs=(
            P(("dp", "expert"), None),
            P(("dp", "expert"), None),
            P("dp", None),
            P("dp", None),
            P("dp", None),
            P("dp", None),
            P("dp"),
            P("dp"),
            P("expert", None, None),
            P("expert", None, None),
        ),
        check_vma=False,
    )
```

time: 1570 us -> 696 us (0.44)
  waiting for transfers between devices: 603 us -> 106 us
  Pallas kernels: 0 us -> 399 us
  blocking collectives: 392 us -> 0 us
  local copies, waits for them, and re-layouts: 300 us -> 56.8 us
  matrix products: 166 us -> 71 us
  other arithmetic: 73.2 us -> 38.8 us
    pallas_call x0 -> x4, Pallas kernels: none -> 399 us  [the longest x1 135 us: scatter_stage(): pl.pallas_call(functools.partial(scatter_kernel, count, dp_count, (local,...]
    all_to_all x2 -> x0, blocking collectives: 331 us -> none  [the longest x1 166 us: shards(): lax.all_to_all(dispatch, 'expert', split_axis=0, concat_axis=1, tiled=True)]
    all_to_all x2 -> x0, waiting for transfers between devices: 297 us -> none  [the longest x1 149 us: shards(): lax.all_to_all(input_grad, 'expert', split_axis=1, concat_axis=0, tiled=T...]
    psum x2 -> x0, waiting for transfers between devices: 267 us -> none  [the longest x1 223 us: shards(): lax.psum(grad_gate_up.astype(jnp.bfloat16), 'dp').astype(jnp.float32)]
    gather x3 -> x0, local copies, waits for them, and re-layouts: 126 us -> none  [the longest x1 62.6 us: shards(): pair_out = returned[flat_expert, clipped].reshape(seq_len, TOP, width_model)]
    all_to_all x10 -> x0, local copies, waits for them, and re-layouts: 96.7 us -> none  [the longest x3 32.2 us: shards(): lax.all_to_all(expert_out, 'expert', split_axis=1, concat_axis=0, tiled=T...]
    reduce_scatter x4 -> x1, waiting for transfers between devices: 11 us -> 101 us  [shards(): lax.psum_scatter(mixture_part, 'expert', scatter_dimension=0, tiled=False)]
    dot_general x10 -> x2, matrix products: 88.1 us -> 0.67 us  [the longest x1 0.35 us: gates_of(): jnp.einsum('...d,de->...e', acts, router, preferred_element_type=jnp.floa...]
  transfers between devices with their start and end apart: 11 -> 2, of which waited for: 7 -> 2; matrix products, arithmetic and copies ran while one was open for 10% -> 7% of each run, Pallas kernels for 0% -> 8%
where the time goes in v1:
time: 696 us; the launch traced here: 687 us
  Pallas kernels  399 us (57%)
  waiting for transfers between devices  106 us (15%)
  matrix products  71 us (10%)
  local copies, waits for them, and re-layouts  56.8 us (8%)
  other arithmetic  38.8 us (6%)
  between operations  15 us (2%)
    pallas_call x1, Pallas kernels, scatter_stage(): pl.pallas_call(functools.partial(scatter_kernel, count, dp_count, (local,...  135 us
    pallas_call x1, Pallas kernels, shared_stage(): pl.pallas_call(functools.partial(shared_kernel, count, dp_count, late, le...  116 us
    reduce_scatter x1, waiting for transfers between devices, shards(): lax.psum_scatter(mixture_part, 'expert', scatter_dimension=0, tiled=False)  101 us
    pallas_call x1, Pallas kernels, expert_stage(): pl.pallas_call(functools.partial(expert_kernel, count), out_shape=(jax.Sh...  91.3 us
    pallas_call x1, Pallas kernels, weights_stage(): pl.pallas_call(functools.partial(weights_kernel, dp_count, count, number)...  57.1 us
    unnamed x99, local copies, waits for them, and re-layouts  24.6 us
    dot_general x1, matrix products, shards(): jnp.einsum('kgqs,skd->qkgd', score_grad, key_rows, preferred_element_type...  16.1 us
    dot_general x1, matrix products, shards(): jnp.einsum('kgqs,qkgd->skd', score_grad, queries, preferred_element_type=...  14.4 us
  transfers between devices with their start and end apart: 2, of which 2 were waited for; matrix products, arithmetic and copies ran while one was open for 7% of the time, Pallas kernels for 8%

profile of v1, /device:TPU:0, one launch (start us, length us, event | category | flops | bytes accessed | tf_op | source)
XLA Modules:
  0.0 687.2 jit_solution(12790357203173134666)
XLA Ops:
  15.6 57.1 %weights_stage.1 = (bf16[4,256,128]{2,1,0:T(8,128)(2,1)S(1)}, bf16[4,256,1024]{2,1,0:T(8,128)(2,1)S(1)}, bf16[4,256,1024]{2,1,0:T(8,128)(2,1)S(1)}, bf16[4,256,1024]{2,1,0:T(8,128)(2,1)S(1)}, f32[8,32,384]{2,1,0:T(8,128)S(1)}) custom-call(bf16[256,128]{1,0:T(8,128)(2,1)S(1)} %maximum_maximum_fusion.1.refs_0_, bf16[256,1024]{1,0:T(8,128)(2,1)S(1)} %copy-done.4, ...), custom_call_target="tpu_custom_call" | custom-call | bytes 104857600 | tf_op jit(solution)/shard_map/weights_stage/pallas_call | solution.py:788
  79.2 2.9 fusion.79
  84.7 2.3 copy.63
  87.2 4.0 copy.64
  95.4 3.3 fusion.35
  99.1 1.6 fusion.10
  100.7 1.9 fusion.4
  102.6 1.7 copy-done.12
  104.3 3.0 fusion.26
  110.7 4.3 all-gather.3.cloned.1.call-done
  114.9 91.3 %expert_stage.1 = (bf16[8,384,1024]{2,1,0:T(8,128)(2,1)}, bf16[8,384,1024]{2,1,0:T(8,128)(2,1)}, f32[8,32,384]{2,1,0:T(8,128)}, bf16[4,896,1024]{2,1,0:T(8,128)(...) custom-call(bf16[384,1024]{1,0:T(8,128)(2,1)} %multiply_convert_fusion.act_ref, ...), custom_call_target="tpu_custom_call" | custom-call | flops 33822867456 | bytes 62914560 | tf_op jit(solution)/shard_map/expert_stage/pallas_call | solution.py:406
  206.2 134.8 %scatter_stage.1 = (f32[384,1024]{1,0:T(8,128)}, f32[32,384]{1,0:T(8,128)}, bf16[2,2,2,384,1024]{4,3,2,1,0:T(8,128)(2,1)}, bf16[2,2,2,384,1024]{4,3,2,1,0:T(8,128)(2,1)}) custom-call(bf16[8,384,1024]{2,1,0:T(8,128)(2,1)} %get-tuple-element.39.refs_0_, f32[8,32,384]{2,1,0:T(8,128)} %get-tuple-element.40.refs_1_, ...), custom_call_target="tpu_custom_call" | custom-call | flops 11274289152 | bytes 209715200 | tf_op jit(solution)/shard_map/scatter_stage/pallas_call | solution.py:982
  344.4 3.1 multiply_reduce_fusion
  349.2 6.2 constant_dynamic-update-slice_fusion.1
  355.4 101.4 %reduce-scatter.2.cloned.1.call-done = bf16[1,384,1024]{2,1,0:T(8,128)(2,1)} async-done(((bf16[8,384,1024]{2,1,0:T(8,128)(2,1)}), bf16[1,384,1024]{2,1,0:T(8,128)(2,1)}) %reduce-scatter.2.cloned.1.call-update) | async-done | bytes 786448 | tf_op jit(solution)/shard_map/reduce_scatter | solution.py:1200
  456.9 3.4 multiply_add_fusion
  461.4 2.6 convolution_convert_fusion.2
  464.4 5.1 fusion.83
  469.5 6.8 fusion.31
  476.3 14.4 %fusion.27 = f32[384,8,64]{0,2,1:T(8,128)S(1)} fusion(f32[8,384,384,2]{2,1,3,0:T(8,128)} %fusion.83, f32[8,2,384]{2,1,0:T(2,128)S(1)} %bitcast.212, f32[8,384,384,2]{2,1,3,0:T(8,128)} %copy-done.12, pred[384,384]{0,1:T(8,128)(4,1)S(1)} %copy-done.29, bf16[384,8,2,32]{0,3,2,1:T(8,128)(2,1)S(1)} %bitcast.202, bf16[384,8,2,32]{0,3,2,1:T(8,128)(2,1)S(1)} %bitcast.200), kind=kOutput, calls=%fused_computation.50 | convolution fusion | flops 329521536 | bytes 20619264 | tf_op jit(solution)/shard_map/kgqs,qkgd->skd/dot_general | solution.py:1229
  490.7 16.1 %fusion.17 = f32[8,64,2,384]{3,1,2,0:T(8,128)} fusion(f32[8,384,384,2]{2,1,3,0:T(8,128)} %fusion.83, f32[8,2,384]{2,1,0:T(2,128)S(1)} %bitcast.213, f32[8,384,384,2]{2,1,3,0:T(8,128)} %copy-done.12, pred[384,384]{0,1:T(8,128)(4,1)S(1)} %copy-done.29, bf16[384,8,32]{0,2,1:T(8,128)(2,1)} %copy-done.37, bf16[384,8,32]{0,2,1:T(8,128)(2,1)S(1)} %copy-done.36), kind=kOutput, calls=%fused_computation.30 | convolution fusion | flops 328735104 | bytes 21012480 | tf_op jit(solution)/shard_map/kgqs,skd->qkgd/dot_general | solution.py:1226
  506.9 1.7 multiply_subtract_fusion
  508.8 2.8 convolution_convert_fusion
  512.7 2.8 convolution_convert_fusion.1
  515.5 2.5 fusion.23
  519.4 115.8 %shared_stage.1 = (f32[8,32,1024]{2,1,0:T(8,128)}, f32[8,32,1024]{2,1,0:T(8,128)}, f32[8,32,1024]{2,1,0:T(8,128)}, f32[8,32,128]{2,1,0:T(8,128)}, bf16[2,2,2,384,1024]{4,3,2,1,0:T(8,128)(2,1)}) custom-call(bf16[4,8,32,1024]{3,2,1,0:T(8,128)(2,1)} %bitcast.179, bf16[4,8,32,1024]{3,2,1,0:T(8,128)(2,1)} %bitcast.186, bf16[4,8,32,1024]{3,2,1,0:T(8,128)(2,1)} %bitcast.185, ...), custom_call_target="tpu_custom_call" | custom-call | bytes 209715200 | tf_op jit(solution)/shard_map/shared_stage/pallas_call | solution.py:1102
  635.2 6.2 constant_dynamic-update-slice_fusion
  641.4 4.8 slice.100
  646.2 8.0 %slice.99 = bf16[4,2,2,256,1024]{4,3,2,1,0:T(8,128)(2,1)} slice(bf16[4,2,2,384,1024]{4,3,2,1,0:T(8,128)(2,1)} %constant_dynamic-update-slice_fusion), slice={[0:4], [0:2], [0:2], [0:256], [0:1024]} | slice | bytes 16777216 | tf_op jit(solution)/shard_map/slice | solution.py:1280
  656.3 6.6 bitcast_convert_fusion.1
  662.9 11.8 %bitcast_convert_fusion = f32[4,1024,1024]{2,1,0:T(8,128)} fusion(bf16[4,2,2,256,1024]{4,3,2,1,0:T(8,128)(2,1)} %slice.99), kind=kLoop, calls=%fused_computation.10 | loop fusion | flops 4194304 | bytes 25165824 | tf_op jit(solution)/shard_map/reshape | solution.py:1280
  674.7 1.6 fusion.22
  (145 shorter events, 40.3 us)
Async XLA Ops:
  7.2 107.8 %all-gather.3.cloned.1.call-start = ((), (), s32[]{:S(2)}) async-start(), calls=%async_computation.2 | async-start | bytes 7077888 | tf_op jit(solution)/shard_map/all_gather | solution.py:1153
  7.9 449.0 %reduce-scatter.2.cloned.1.call-start = ((), (), s32[]{:S(2)}) async-start(), calls=%async_computation.1 | async-start | bytes 7077888 | tf_op jit(solution)/shard_map/reduce_scatter | solution.py:1200
  10.4 2.0 copy-start.40
  75.4 6.7 copy-start.9
  75.4 32.0 %copy-start = (bf16[4,256,1024]{2,1,0:T(8,128)(2,1)}, bf16[4,256,1024]{2,1,0:T(8,128)(2,1)S(1)}, u32[]{:S(2)}) copy-start(bf16[4,256,1024]{2,1,0:T(8,128)(2,1)S(1)} %get-tuple-element.36) | copy-start | bytes 6291460
  82.8 4.2 copy-start.18
  87.2 4.0 copy-start.42
  94.0 4.8 copy-start.20
  94.1 8.5 %copy-start.28 = (pred[384,384]{0,1:T(8,128)(4,1)}, pred[384,384]{0,1:T(8,128)(4,1)S(1)}, u32[]{:S(2)}) copy-start(pred[384,384]{0,1:T(8,128)(4,1)S(1)} %fusion.37) | copy-start | bytes 442372
  95.4 3.6 copy-start.35
  95.4 3.6 copy-start.37
  100.7 3.6 copy-start.12
  104.3 3.0 copy-start.14
  341.1 2.1 copy-start.38
  342.2 2.2 copy-start.11
  456.9 3.4 copy-start.1
  464.3 5.1 copy-start.29
  464.3 5.1 copy-start.39
  469.5 6.8 copy-start.32
  469.5 6.8 copy-start.34
  476.3 14.4 %copy-start.36 = (bf16[384,8,32]{0,2,1:T(8,128)(2,1)S(1)}, bf16[384,8,32]{0,2,1:T(8,128)(2,1)}, u32[]{:S(2)}) copy-start(bf16[384,8,32]{0,2,1:T(8,128)(2,1)} %copy-done.35) | copy-start | bytes 589828
  490.6 16.2 %copy-start.21 = (f32[384,32]{0,1:T(8,128)S(1)}, f32[384,32]{0,1:T(8,128)}, u32[]{:S(2)}) copy-start(f32[384,32]{0,1:T(8,128)} %copy-done.20) | copy-start | bytes 147460
  490.7 16.2 %copy-start.30 = (f32[384,32]{0,1:T(8,128)S(1)}, f32[384,32]{0,1:T(8,128)}, u32[]{:S(2)}) copy-start(f32[384,32]{0,1:T(8,128)} %get-tuple-element.76) | copy-start | bytes 147460
  506.9 1.8 copy-start.15
  508.7 2.8 copy-start.3
  512.6 2.8 copy-start.8
  515.4 2.9 copy-start.26
  515.4 2.9 copy-start.27
  515.5 2.9 copy-start.41
  646.2 8.0 %copy-start.22 = (f32[8,32,128]{2,1,0:T(8,128)S(1)}, f32[8,32,128]{2,1,0:T(8,128)}, u32[]{:S(2)}) copy-start(f32[8,32,128]{2,1,0:T(8,128)} %get-tuple-element.53) | copy-start | bytes 393220
  662.9 11.8 %copy-start.19 = (f32[384,1024]{1,0:T(8,128)S(1)}, f32[384,1024]{1,0:T(8,128)}, u32[]{:S(2)}) copy-start(f32[384,1024]{1,0:T(8,128)} %get-tuple-element.87) | copy-start | bytes 4718596
  676.3 2.6 copy-start.23
  (14 other events, 17.8 us)
Sparse Core Ops, SparseCore 0:
  10.2 104.7 all-gather.2
  341.2 115.5 reduce-scatter.1
